TPU v7x, 256 devices: a whole 4x4x8 slice. The times are simulated.
256 devices in a mesh: pair: 64 (over z, x, core), sp: 4 (over y).
Axes of the slice: x: 4, y: 4, z: 8, core: 2. Of those that a mesh axis runs over, the one named last changes fastest.
Arguments:
- gamma_pairs: bfloat16 [2, 64, 128, 30720], P(None, None, 'sp', 'pair'), may hold values from -6 to 6
- occ_coef: bfloat16 [30720, 128], P(None, 'sp'), may hold values from -0.5 to 0.5
- block_lists: int32 [4, 4, 20], replicated, may hold values from 0 to 79, as said below
- block_counts: int32 [4, 4], replicated, may hold values from 1 to 20, as said below
- block_coords: int32 [320, 2], replicated, may hold values from 0 to 239, as said below
Outputs:
- ao_gamma: bfloat16 [2, 64, 320, 128, 128], P(None, 'pair', 'sp')
Inputs may be any that keep to these rules, and one draw needn't show every extreme that they name: `block_lists`: the 20 entries of one list are distinct; entries past block_counts are not used. `block_counts`: in every draw some owner gets 20 blocks from every slab. `block_coords`: every one of the 240 column blocks is the column block of some shell-pair block.
All inputs are finite; a program needn't handle non-finite values.
Results may differ from a plain program's by a relative error of at most 0.0039.
Values may be sent and summed in bfloat16 or wider, within the bound.
No kernel may reach another device: no remote copies, remote signals or barrier semaphores. Data moves between devices by JAX's collectives and lax.ppermute only.
A program may use at most 128 MiB of HBM per device.

v0:
```python
import functools

import jax
import jax.numpy as jnp
from jax import lax
from jax.experimental import pallas as pl
from jax.experimental.pallas import tpu as pltpu
from jax.sharding import Mesh, PartitionSpec as P

BLK = 128
NZ, NX, NCORE = 8, 4, 2
LEVELS = (5, 6, 8)
BF = jnp.bfloat16
VMEM = pl.BlockSpec(memory_space=pltpu.VMEM)
ANY = pl.BlockSpec(memory_space=pl.ANY)
SMEM = pl.BlockSpec(memory_space=pltpu.SMEM)


def params(mib):
    return pltpu.CompilerParams(vmem_limit_bytes=mib << 20)


def cost(nbytes, flops=0):
    return pl.CostEstimate(flops=flops, bytes_accessed=nbytes, transcendentals=0)


def turn(start, k, n):
    at = start + k
    at = jnp.where(at >= n, at - n, at)
    return jnp.where(at < 0, at + n, at)


def coef_pick_kernel(me, rows, coef, after, *outs):
    slots = outs[0].shape[0]
    for k, out in enumerate(outs):
        base = turn(me[0], k, len(outs)) * slots

        def step(t, _):
            start = pl.multiple_of(rows[base + t] * BLK, BLK)
            out[t] = coef[:, pl.ds(start, BLK)]
            return 0

        lax.fori_loop(0, slots, step, 0, unroll=4)


def coef_pick(me, coef_t, rows, after, groups):
    slots, occ = rows.shape[0] // groups, coef_t.shape[0]
    return pl.pallas_call(
        coef_pick_kernel,
        out_shape=[jax.ShapeDtypeStruct((slots, occ, BLK), BF)] * groups,
        in_specs=[SMEM, SMEM, VMEM, ANY],
        out_specs=[VMEM] * groups,
        compiler_params=params(16),
        cost_estimate=cost(4 << 20),
        name="coef_pick",
    )(me, rows, coef_t, after)


def coef_join_kernel(me, pos, *rest):
    pieces, out, held = rest[:-2], rest[-2], rest[-1]
    groups, owned = len(pieces), out.shape[0]
    for k, piece in enumerate(pieces):
        held[turn(me[0], -k, groups)] = piece[...]

    def step(k, _):
        parts = []
        for s in range(groups):
            p = pos[s * owned + k]
            block = held[s, jnp.maximum(p, 0)]
            parts.append(jnp.where(p >= 0, block, jnp.zeros_like(block)))
        out[k] = jnp.concatenate(parts, axis=0).T
        return 0

    lax.fori_loop(0, owned, step, 0)


def coef_join(me, pieces, pos, owned):
    groups = len(pieces)
    slots, occ, _ = pieces[0].shape
    return pl.pallas_call(
        coef_join_kernel,
        out_shape=jax.ShapeDtypeStruct((owned, BLK, groups * occ), BF),
        in_specs=[SMEM, SMEM] + [VMEM] * groups,
        out_specs=VMEM,
        scratch_shapes=[pltpu.VMEM((groups, slots, occ, BLK), BF)],
        compiler_params=params(16),
        cost_estimate=cost(4 << 20),
        name="coef_join",
    )(me, pos, *pieces)


def core_split_kernel(batch, at, pairs, *rest):
    outs, sems = rest[:-1], rest[-1]
    copies = []
    for k, out in enumerate(outs):
        core = at[1] if k == 0 else 1 - at[1]
        copies.append(pltpu.make_async_copy(pairs.at[batch, :, :, core], out, sems.at[k]))
    for copy in copies:
        copy.start()
    for copy in copies:
        copy.wait()


def core_split(batch, at, pairs):
    _, nz, nx, _, occ, width = pairs.shape
    return pl.pallas_call(
        functools.partial(core_split_kernel, batch),
        out_shape=[jax.ShapeDtypeStruct((nz, nx, occ, width), BF)] * 2,
        in_specs=[SMEM, pl.BlockSpec(memory_space=pltpu.HBM)],
        out_specs=[VMEM] * 2,
        scratch_shapes=[pltpu.SemaphoreType.DMA((2,))],
        compiler_params=params(12),
        cost_estimate=cost(4 << 20),
        name=f"core_split{batch}",
    )(at, pairs)


def cut_tile(odd, t, left, right, out, j):
    rows, occ, width = left.shape
    lo = t * BLK - (BLK // 2 if odd else 0)
    first, last = max(lo, 0), min(lo + BLK, 2 * width)

    def row(i, _):
        parts = []
        if lo < 0:
            parts.append(jnp.zeros((occ, -lo), BF))
        if first < width:
            parts.append(left[i, :, first : min(last, width)])
        if last > width:
            parts.append(right[i, :, max(first, width) - width : last - width])
        if last < lo + BLK:
            parts.append(jnp.zeros((occ, lo + BLK - last), BF))
        to = i % NX * NZ + i // NX
        out[to, j] = parts[0] if len(parts) == 1 else jnp.concatenate(parts, axis=1)
        return 0

    lax.fori_loop(0, rows, row, 0)


def tile_pick_kernel(at, listed, own, got, after, out):
    held = listed.shape[0] - 1
    for odd in (0, 1):
        for core in (0, 1):
            left, right = (own, got) if core == 0 else (got, own)

            @pl.when((at[0] % 2 == odd) & (at[1] == core))
            def _():
                def keep(j, _):
                    for t in range(held):

                        @pl.when(listed[j] == t)
                        def _():
                            cut_tile(odd, t, left, right, out, j)

                    return 0

                lax.fori_loop(0, jnp.minimum(listed[held], out.shape[1]), keep, 0)


def tile_pick(at, listed, own, got, after, cap):
    rows, occ, width = own.shape
    return pl.pallas_call(
        tile_pick_kernel,
        out_shape=jax.ShapeDtypeStruct((rows, cap, occ, BLK), BF),
        in_specs=[SMEM, SMEM, VMEM, VMEM, ANY],
        out_specs=VMEM,
        compiler_params=params(16),
        cost_estimate=cost(4 << 20),
        name="tile_pick",
    )(at, listed, own, got, after)


def slot_pick_kernel(me, spots, got, *outs):
    slots, occ, _ = outs[0].shape
    low = lax.broadcasted_iota(jnp.int32, (occ, BLK), 1) < BLK // 2
    total = len(outs) * slots
    for k, out in enumerate(outs):
        base = turn(me[0], k, len(outs)) * slots

        def step(t, _):
            a, b = spots[base + t], spots[total + base + t]
            out[t] = jnp.where(low, got[a >> 3, a & 7], got[b >> 3, b & 7])
            return 0

        lax.fori_loop(0, slots, step, 0, unroll=5)


def slot_pick(me, spots, got, groups):
    slots = spots.shape[0] // (2 * groups)
    occ = got.shape[2]
    return pl.pallas_call(
        slot_pick_kernel,
        out_shape=[jax.ShapeDtypeStruct((slots, occ, BLK), BF)] * groups,
        in_specs=[SMEM, SMEM, VMEM],
        out_specs=[VMEM] * groups,
        compiler_params=params(16),
        cost_estimate=cost(2 << 20),
        name="slot_pick",
    )(me, spots, got)


def product_kernel(per, groups, me, pos, coef, *rest):
    gamma, (out, held) = rest[:groups], rest[-2:]
    owned = pos.shape[0] // groups
    step = pl.program_id(0)

    @pl.when(step == 0)
    def _():
        for k in range(groups):
            held[turn(me[0], -k, groups)] = gamma[k][...]

    for j in range(per):
        at = [jnp.maximum(pos[s * owned + step * per + j], 0) for s in range(groups)]
        cols = jnp.concatenate([held[s, at[s]] for s in range(groups)], axis=0)
        total = jnp.dot(coef[j], cols, preferred_element_type=jnp.float32)
        out[0, 0, j] = total.astype(BF)


def product(batch, batches, me, coef, gamma, pos, prior):
    owned = coef.shape[0]
    groups = len(gamma)
    per = 20
    extra = [] if prior is None else [prior]
    return pl.pallas_call(
        functools.partial(product_kernel, per, groups),
        out_shape=jax.ShapeDtypeStruct((batches, 1, owned, BLK, BLK), BF),
        grid_spec=pltpu.PrefetchScalarGridSpec(
            num_scalar_prefetch=2,
            grid=(owned // per,),
            in_specs=[pl.BlockSpec((per, BLK, coef.shape[2]), lambda i, *_: (i, 0, 0))]
            + [pl.BlockSpec(gamma[0].shape, lambda i, *_: (0, 0, 0))] * groups
            + [ANY] * len(extra),
            out_specs=pl.BlockSpec((1, 1, per, BLK, BLK), lambda i, *_: (batch, 0, i, 0, 0)),
            scratch_shapes=[pltpu.VMEM((groups,) + gamma[0].shape, BF)],
        ),
        input_output_aliases={3 + groups: 0} if extra else {},
        compiler_params=params(16),
        cost_estimate=cost(6 << 20, 2 * owned * BLK**3),
        name=f"product{batch}",
    )(me, pos, coef, *gamma, *extra)


def local(gamma_pairs, occ_coef, block_lists, block_counts, block_coords):
    batches, aux, occ, width = gamma_pairs.shape
    groups = lax.axis_size("sp")
    basis = occ_coef.shape[0]
    nblk = basis // BLK
    total_blocks = block_coords.shape[0]
    owned = total_blocks // groups
    capacity = block_lists.shape[2]
    me_s = lax.axis_index("sp")
    me_z = lax.axis_index("z")

    at = jnp.stack([lax.axis_index("x"), lax.axis_index("core")]).astype(jnp.int32)
    pairs = gamma_pairs.reshape(batches, NZ, NX, NCORE, occ, width)

    pairs = pltpu.with_memory_space_constraint(pairs, pltpu.HBM)

    def swap(halves):
        return halves[0], lax.ppermute(halves[1], "core", [(0, 1), (1, 0)])

    split0, block_lists, block_counts, block_coords = lax.optimization_barrier(
        (core_split(0, at, pairs), block_lists, block_counts, block_coords)
    )
    halves0 = swap(split0)

    valid = jnp.arange(capacity, dtype=jnp.int32)[None, None, :] < block_counts[:, :, None]
    lists = jnp.clip(block_lists, 0, owned - 1)
    ids = lists + (jnp.arange(groups, dtype=jnp.int32) * owned)[None, :, None]
    hit = ids.reshape(groups, -1, 1) == jnp.arange(total_blocks, dtype=jnp.int32)
    row_ids = jnp.sum(jnp.where(hit, block_coords[:, 0], 0), axis=2)
    col_ids = jnp.sum(jnp.where(hit, block_coords[:, 1], 0), axis=2)
    live_col = jnp.where(valid.reshape(groups, -1), col_ids, -1)
    need = jnp.any(live_col[:, :, None] == jnp.arange(nblk, dtype=jnp.int32), axis=1)
    pair_blocks = 2 * nblk // (NZ * NX)
    held = -(-2 * width // BLK)
    need = need.reshape(groups, NZ * NX // 2, 1, pair_blocks).astype(jnp.int32)
    need = jnp.concatenate([need[..., :held], need[..., pair_blocks - held :]], axis=2)
    need = need.reshape(groups, NZ * NX, held)
    most = jnp.max(jnp.sum(need, axis=2))
    my_need = lax.dynamic_index_in_dim(need, me_s, 0, keepdims=False)
    tile_ids = jnp.arange(held, dtype=jnp.int32)
    before = (tile_ids[None, :] < tile_ids[:, None]).astype(jnp.int32)
    rank = jnp.sum(my_need[:, None, :] * before[None], axis=2)
    my_cols = lax.dynamic_index_in_dim(col_ids, me_s, 0, keepdims=False)
    my_rows = lax.dynamic_index_in_dim(row_ids, me_s, 0, keepdims=False)
    my_live = lax.dynamic_index_in_dim(valid.reshape(groups, -1), me_s, 0, keepdims=False)
    slot_cols = my_cols.reshape(groups, capacity)
    slot_cols = jnp.where(my_live.reshape(groups, capacity), slot_cols, slot_cols[:, :1])
    slot_cols = slot_cols.reshape(-1)
    two_chips, within = slot_cols // pair_blocks, slot_cols % pair_blocks
    upper = jnp.arange(2, dtype=jnp.int32)[:, None]
    on_odd = (within[None, :] > held - 1 - upper).astype(jnp.int32)
    chip = 2 * two_chips[None, :] + on_odd
    tile = within[None, :] - on_odd * (pair_blocks - held)
    tile_hit = (chip * held + tile)[:, :, None] == jnp.arange(NZ * NX * held, dtype=jnp.int32)
    order = jnp.sum(jnp.where(tile_hit, rank.reshape(-1), 0), axis=2)
    spots = (8 * (chip % NX * NZ + chip // NX) + order).reshape(-1)
    my_chip = me_z * NX + lax.axis_index("x")
    chip_need = lax.dynamic_index_in_dim(my_need, my_chip, 0, keepdims=False)
    chip_rank = lax.dynamic_index_in_dim(rank, my_chip, 0, keepdims=False)
    listed = jnp.sum(
        jnp.where(
            (chip_rank[None, :] == tile_ids[:, None]) & (chip_need[None, :] > 0),
            tile_ids[None, :],
            0,
        ),
        axis=1,
    )
    listed = jnp.concatenate([listed, jnp.sum(chip_need, keepdims=True)])
    to_me = lax.dynamic_index_in_dim(lists, me_s, 1, keepdims=False)
    to_me_valid = lax.dynamic_index_in_dim(valid, me_s, 1, keepdims=False)
    hits = (to_me[:, None, :] == jnp.arange(owned, dtype=jnp.int32)[None, :, None]) & to_me_valid[
        :, None, :
    ]
    slot_no = jnp.arange(capacity, dtype=jnp.int32) + 1
    pos = (jnp.sum(jnp.where(hits, slot_no, 0), axis=2) - 1).reshape(-1)

    me = me_s[None].astype(jnp.int32)
    def exchange_owners(sent):
        return [sent[0]] + [
            lax.ppermute(sent[k], "sp", [(i, (i + k) % groups) for i in range(groups)])
            for k in range(1, groups)
        ]

    def finish(cap, halves0, pairs, coef_t, my_rows, pos, listed, spots):
        def tiles(halves, after):
            halves = [half.reshape(NZ * NX, occ, width) for half in halves]
            picked = tile_pick(at, listed, *halves, after, cap)
            return picked, lax.all_to_all(picked, ("x", "z"), 0, 0, tiled=True)

        def owners(got):
            return exchange_owners(slot_pick(me, spots, got, groups))

        picked0, got0 = tiles(halves0, me)
        coef_parts = exchange_owners(coef_pick(me, coef_t, my_rows, picked0, groups))
        coef = coef_join(me, coef_parts, pos, owned)
        _, got1 = tiles(swap(core_split(1, at, pairs)), coef)
        out = product(0, batches, me, coef, owners(got0), pos, None)
        return product(1, batches, me, coef, owners(got1), pos, out)

    level = sum((most > cap).astype(jnp.int32) for cap in LEVELS[:-1])
    level, *tables = lax.optimization_barrier((level, my_rows, pos, listed, spots))
    branches = [functools.partial(finish, cap) for cap in LEVELS]
    return lax.switch(level, branches, halves0, pairs, occ_coef.T, *tables)


def solution(mesh):
    groups = mesh.shape["sp"]
    grid = Mesh(mesh.devices.reshape(NZ, NX, NCORE, groups), ("z", "x", "core", "sp"))
    pair = ("z", "x", "core")
    in_specs = (P(None, None, "sp", pair), P(None, "sp"), P(), P(), P())
    out_specs = P(None, pair, "sp", None, None)
    return jax.shard_map(local, mesh=grid, in_specs=in_specs, out_specs=out_specs, check_vma=False)
```

profile of v0, /device:TPU:34, one launch (start us, length us, event | category | flops | bytes accessed | tf_op | source)
XLA Modules:
  0.0 120.9 jit_solution(3619098032400978087)
XLA Ops:
  0.1 3.1 %core_split0.1 = (bf16[8,4,32,480]{3,2,1,0:T(8,128)(2,1)}, bf16[8,4,32,480]{3,2,1,0:T(8,128)(2,1)S(1)}) custom-call(s32[2]{0:T(128)S(1)} %pad_add_fusion.1.at, bf16[2,8,4,2,32,480]{5,4,3,2,1,0:T(8,128)(2,1)} %bitcast.39), custom_call_target="tpu_custom_call" | custom-call | bytes 4194304 | tf_op jit(solution)/shard_map/core_split0/pallas_call | solution.py:106
  10.3 110.6 %conditional.1 = (bf16[2,1,80,128,128]{4,3,2,1,0:T(8,128)(2,1)}) conditional(s32[]{:T(128)} %clamp.10, (bf16[8,4,32,480]{3,2,1,0:T(8,128)(2,1)}, bf16[8,4,32,480]{3,2,1,0:T(8,128)(2,1)}, s32[2]{0:T(128)S(1)}, s32[9]{0:T(128)S(1)}, s32[]{:T(128)}, /*index=5*/s32[80]{0:T(128)S(1)}, bf16[32,30720]{1,0:T(8,128)(2,1)S(1)}, ...), branch_computations={%region_10.11_spmd, %region_11.12_spmd, %region_12.13_spmd} | conditional | flops 671088640 | bytes 68551160 | solution.py:345
  10.3 9.7 %tile_pick.6.after = bf16[32,5,32,128]{3,2,1,0:T(8,128)(2,1)} custom-call(s32[2]{0:T(128)S(1)} %get-tuple-element.73.at, s32[9]{0:T(128)S(1)} %get-tuple-element.74.listed, bf16[32,32,480]{2,1,0:T(8,128)(2,1)} %bitcast.46, bf16[32,32,480]{2,1,0:T(8,128)(2,1)} %bitcast.2.got, s32[1]{0:T(128)} %bitcast.after.me), custom_call_target="tpu_custom_call" | custom-call | bytes 4194304 | tf_op jit(solution)/shard_map/cond/branch_0_fun/tile_pick/pallas_call | solution.py:162
  20.1 7.0 %all-to-all-start.1 = ((bf16[32,5,32,128]{3,2,1,0:T(8,128)(2,1)}), bf16[32,5,32,128]{3,2,1,0:T(8,128)(2,1)}, u32[]{:S(2)}, u32[]{:S(2)}) async-start(bf16[32,5,32,128]{3,2,1,0:T(8,128)(2,1)} %tile_pick.6.after), calls=%async_computation.1 | async-start | bytes 2621440 | tf_op jit(solution)/shard_map/cond/branch_0_fun/all_to_all | solution.py:330
  27.1 2.1 %core_split1.3 = (bf16[8,4,32,480]{3,2,1,0:T(8,128)(2,1)S(1)}, bf16[8,4,32,480]{3,2,1,0:T(8,128)(2,1)S(1)}) custom-call(s32[2]{0:T(128)S(1)} %get-tuple-element.73.at, bf16[2,8,4,2,32,480]{5,4,3,2,1,0:T(8,128)(2,1)} %get-tuple-element.82.pairs), custom_call_target="tpu_custom_call" | custom-call | bytes 4194304 | tf_op jit(solution)/shard_map/cond/branch_0_fun/core_split1/pallas_call | solution.py:106
  30.2 5.7 %collective-permute-start = (bf16[20,32,128]{2,1,0:T(8,128)(2,1)S(1)}, bf16[20,32,128]{2,1,0:T(8,128)(2,1)S(1)}, u32[]{:S(2)}, u32[]{:S(2)}) collective-permute-start(bf16[20,32,128]{2,1,0:T(8,128)(2,1)S(1)} %get-tuple-element.78), channel_id=1, source_target_pairs={{0,1},{1,2},{2,3},{3,0},{4,5},{5,6},{6,7},{7,4},{8,9},{9,10},{10,1... | collective-permute-start | bytes 491528 | tf_op jit(solution)/shard_map/cond/branch_0_fun/ppermute | solution.py:322
  35.9 2.9 %collective-permute-start.1 = (bf16[20,32,128]{2,1,0:T(8,128)(2,1)S(1)}, bf16[20,32,128]{2,1,0:T(8,128)(2,1)S(1)}, u32[]{:S(2)}, u32[]{:S(2)}) collective-permute-start(bf16[20,32,128]{2,1,0:T(8,128)(2,1)S(1)} %get-tuple-element.79), channel_id=1, source_target_pairs={{0,2},{1,3},{2,0},{3,1},{4,6},{5,7},{6,4},{7,5},{8,10},{9,11},{10,... | collective-permute-start | bytes 491528 | tf_op jit(solution)/shard_map/cond/branch_0_fun/ppermute | solution.py:322
  38.8 1.9 %collective-permute-start.2 = (bf16[20,32,128]{2,1,0:T(8,128)(2,1)S(1)}, bf16[20,32,128]{2,1,0:T(8,128)(2,1)S(1)}, u32[]{:S(2)}, u32[]{:S(2)}) collective-permute-start(bf16[20,32,128]{2,1,0:T(8,128)(2,1)S(1)} %get-tuple-element.80), channel_id=1, source_target_pairs={{0,3},{1,0},{2,1},{3,2},{4,7},{5,4},{6,5},{7,6},{8,11},{9,8},{10,9... | collective-permute-start | bytes 491528 | tf_op jit(solution)/shard_map/cond/branch_0_fun/ppermute | solution.py:322
  40.6 1.5 %collective-permute-done.rest_1_ = bf16[20,32,128]{2,1,0:T(8,128)(2,1)S(1)} collective-permute-done((bf16[20,32,128]{2,1,0:T(8,128)(2,1)S(1)}, bf16[20,32,128]{2,1,0:T(8,128)(2,1)S(1)}, u32[]{:S(2)}, u32[]{:S(2)}) %collective-permute-start) | collective-permute-done | bytes 163872 | tf_op jit(solution)/shard_map/cond/branch_0_fun/ppermute | solution.py:322
  42.2 4.7 %collective-permute-done.1.rest_2_ = bf16[20,32,128]{2,1,0:T(8,128)(2,1)S(1)} collective-permute-done((bf16[20,32,128]{2,1,0:T(8,128)(2,1)S(1)}, bf16[20,32,128]{2,1,0:T(8,128)(2,1)S(1)}, u32[]{:S(2)}, u32[]{:S(2)}) %collective-permute-start.1) | collective-permute-done | bytes 163872 | tf_op jit(solution)/shard_map/cond/branch_0_fun/ppermute | solution.py:322
  46.8 6.4 %coef_join.3.after.coef = bf16[80,128,128]{2,1,0:T(8,128)(2,1)S(1)} custom-call(s32[1]{0:T(128)} %bitcast.after.me, s32[320]{0:T(512)S(1)} %get-tuple-element.70.pos, bf16[20,32,128]{2,1,0:T(8,128)(2,1)S(1)} %get-tuple-element.77.rest_0_, bf16[20,32,128]{2,1,0:T(8,128)(2,1)S(1)} %collective-permute-done.rest_1_, ...), custom_call_target="tpu_custom_call" | custom-call | bytes 4194304 | tf_op jit(solution)/shard_map/cond/branch_0_fun/coef_join/pallas_call | solution.py:80
  53.3 7.6 %tile_pick.7 = bf16[32,5,32,128]{3,2,1,0:T(8,128)(2,1)S(1)} custom-call(s32[2]{0:T(128)S(1)} %get-tuple-element.73.at, s32[9]{0:T(128)S(1)} %get-tuple-element.74.listed, bf16[32,32,480]{2,1,0:T(8,128)(2,1)S(1)} %bitcast.33, bf16[32,32,480]{2,1,0:T(8,128)(2,1)S(1)} %bitcast.34, bf16[80,128,128]{2,1,0:T(8,128)(2,1)S(1)} %coef_join.3.after.coef), custom_call_target="tpu_custom_call" | custom-call | bytes 4194304 | tf_op jit(solution)/shard_map/cond/branch_0_fun/tile_pick/pallas_call | solution.py:162
  62.0 6.6 %all-to-all-start = ((bf16[32,5,32,128]{3,2,1,0:T(8,128)(2,1)}), bf16[32,5,32,128]{3,2,1,0:T(8,128)(2,1)}, u32[]{:S(2)}, u32[]{:S(2)}) async-start(bf16[32,5,32,128]{3,2,1,0:T(8,128)(2,1)} %copy-done.2), calls=%async_computation | async-start | bytes 2621440 | tf_op jit(solution)/shard_map/cond/branch_0_fun/all_to_all | solution.py:330
  68.6 2.6 %slot_pick.7 = (bf16[20,32,128]{2,1,0:T(8,128)(2,1)S(1)}, bf16[20,32,128]{2,1,0:T(8,128)(2,1)}, bf16[20,32,128]{2,1,0:T(8,128)(2,1)}, bf16[20,32,128]{2,1,0:T(8,128)(2,1)S(1)}) custom-call(s32[1]{0:T(128)} %bitcast.after.me, s32[160]{0:T(256)S(1)} %get-tuple-element.81.spots, bf16[32,5,32,128]{3,2,1,0:T(8,128)(2,1)} %all-to-all-done.1.got), custom_call_target="tpu_custom_call" | custom-call | bytes 2097152 | tf_op jit(solution)/shard_map/cond/branch_0_fun/slot_pick/pallas_call | solution.py:191
  71.2 4.1 %collective-permute-start.7 = (bf16[20,32,128]{2,1,0:T(8,128)(2,1)}, bf16[20,32,128]{2,1,0:T(8,128)(2,1)S(1)}, u32[]{:S(2)}, u32[]{:S(2)}) collective-permute-start(bf16[20,32,128]{2,1,0:T(8,128)(2,1)} %get-tuple-element.90), channel_id=1, source_target_pairs={{0,1},{1,2},{2,3},{3,0},{4,5},{5,6},{6,7},{7,4},{8,9},{9,10},{10,1... | collective-permute-start | bytes 491528 | tf_op jit(solution)/shard_map/cond/branch_0_fun/ppermute | solution.py:322
  75.4 2.9 %collective-permute-start.8 = (bf16[20,32,128]{2,1,0:T(8,128)(2,1)}, bf16[20,32,128]{2,1,0:T(8,128)(2,1)S(1)}, u32[]{:S(2)}, u32[]{:S(2)}) collective-permute-start(bf16[20,32,128]{2,1,0:T(8,128)(2,1)} %get-tuple-element.91), channel_id=1, source_target_pairs={{0,2},{1,3},{2,0},{3,1},{4,6},{5,7},{6,4},{7,5},{8,10},{9,11},{10,... | collective-permute-start | bytes 491528 | tf_op jit(solution)/shard_map/cond/branch_0_fun/ppermute | solution.py:322
  78.3 2.3 %collective-permute-start.9 = (bf16[20,32,128]{2,1,0:T(8,128)(2,1)S(1)}, bf16[20,32,128]{2,1,0:T(8,128)(2,1)S(1)}, u32[]{:S(2)}, u32[]{:S(2)}) collective-permute-start(bf16[20,32,128]{2,1,0:T(8,128)(2,1)S(1)} %get-tuple-element.92), channel_id=1, source_target_pairs={{0,3},{1,0},{2,1},{3,2},{4,7},{5,4},{6,5},{7,6},{8,11},{9,8},{10,9... | collective-permute-start | bytes 491528 | tf_op jit(solution)/shard_map/cond/branch_0_fun/ppermute | solution.py:322
  80.6 21.2 %all-to-all-done.got = bf16[32,5,32,128]{3,2,1,0:T(8,128)(2,1)} async-done(((bf16[32,5,32,128]{3,2,1,0:T(8,128)(2,1)}), bf16[32,5,32,128]{3,2,1,0:T(8,128)(2,1)}, u32[]{:S(2)}, u32[]{:S(2)}) %all-to-all-start) | async-done | bytes 1310752 | tf_op jit(solution)/shard_map/cond/branch_0_fun/all_to_all | solution.py:330
  101.8 1.9 %slot_pick.6 = (bf16[20,32,128]{2,1,0:T(8,128)(2,1)S(1)}, bf16[20,32,128]{2,1,0:T(8,128)(2,1)S(1)}, bf16[20,32,128]{2,1,0:T(8,128)(2,1)S(1)}, bf16[20,32,128]{2,1,0:T(8,128)(2,1)S(1)}) custom-call(s32[1]{0:T(128)} %bitcast.after.me, s32[160]{0:T(256)S(1)} %get-tuple-element.81.spots, bf16[32,5,32,128]{3,2,1,0:T(8,128)(2,1)} %all-to-all-done.got), custom_call_target="tpu_custom_call" | custom-call | bytes 2097152 | tf_op jit(solution)/shard_map/cond/branch_0_fun/slot_pick/pallas_call | solution.py:191
  103.7 4.2 %collective-permute-start.4 = (bf16[20,32,128]{2,1,0:T(8,128)(2,1)S(1)}, bf16[20,32,128]{2,1,0:T(8,128)(2,1)S(1)}, u32[]{:S(2)}, u32[]{:S(2)}) collective-permute-start(bf16[20,32,128]{2,1,0:T(8,128)(2,1)S(1)} %get-tuple-element.86), channel_id=1, source_target_pairs={{0,1},{1,2},{2,3},{3,0},{4,5},{5,6},{6,7},{7,4},{8,9},{9,10},{10,1... | collective-permute-start | bytes 491528 | tf_op jit(solution)/shard_map/cond/branch_0_fun/ppermute | solution.py:322
  107.9 2.9 %collective-permute-start.5 = (bf16[20,32,128]{2,1,0:T(8,128)(2,1)S(1)}, bf16[20,32,128]{2,1,0:T(8,128)(2,1)S(1)}, u32[]{:S(2)}, u32[]{:S(2)}) collective-permute-start(bf16[20,32,128]{2,1,0:T(8,128)(2,1)S(1)} %get-tuple-element.87), channel_id=1, source_target_pairs={{0,2},{1,3},{2,0},{3,1},{4,6},{5,7},{6,4},{7,5},{8,10},{9,11},{10,... | collective-permute-start | bytes 491528 | tf_op jit(solution)/shard_map/cond/branch_0_fun/ppermute | solution.py:322
  110.8 2.1 %collective-permute-start.6 = (bf16[20,32,128]{2,1,0:T(8,128)(2,1)S(1)}, bf16[20,32,128]{2,1,0:T(8,128)(2,1)S(1)}, u32[]{:S(2)}, u32[]{:S(2)}) collective-permute-start(bf16[20,32,128]{2,1,0:T(8,128)(2,1)S(1)} %get-tuple-element.88), channel_id=1, source_target_pairs={{0,3},{1,0},{2,1},{3,2},{4,7},{5,4},{6,5},{7,6},{8,11},{9,8},{10,9... | collective-permute-start | bytes 491528 | tf_op jit(solution)/shard_map/cond/branch_0_fun/ppermute | solution.py:322
  112.9 3.3 %product0.3.rest_4_ = bf16[2,1,80,128,128]{4,3,2,1,0:T(8,128)(2,1)} custom-call(s32[1]{0:T(128)} %bitcast.after.me, s32[320]{0:T(512)S(1)} %get-tuple-element.70.pos, bf16[80,128,128]{2,1,0:T(8,128)(2,1)S(1)} %coef_join.3.after.coef, bf16[20,32,128]{2,1,0:T(8,128)(2,1)S(1)} %get-tuple-element.89.rest_0_, ...), custom_call_target="tpu_custom_call" | custom-call | flops 335544320 | bytes 6291456 | tf_op jit(solution)/shard_map/cond/branch_0_fun/product0/pallas_call | solution.py:224
  117.6 3.3 %product1.3 = bf16[2,1,80,128,128]{4,3,2,1,0:T(8,128)(2,1)} custom-call(s32[1]{0:T(128)} %bitcast.after.me, s32[320]{0:T(512)S(1)} %get-tuple-element.70.pos, bf16[80,128,128]{2,1,0:T(8,128)(2,1)S(1)} %coef_join.3.after.coef, bf16[20,32,128]{2,1,0:T(8,128)(2,1)S(1)} %get-tuple-element.85.rest_0_, ...), custom_call_target="tpu_custom_call", output_to_operand_aliasing={{}: (7, {})} | custom-call | flops 335544320 | bytes 6291456 | tf_op jit(solution)/shard_map/cond/branch_0_fun/product1/pallas_call | solution.py:224
  (76 shorter events, 9.1 us)
Async XLA Ops:
  0.1 3.4 %copy-start.5 = (s32[4,4]{1,0:T(4,128)S(1)}, s32[4,4]{1,0:T(4,128)}, u32[]{:S(2)}) copy-start(s32[4,4]{1,0:T(4,128)} %param.11) | copy-start | bytes 196
  0.1 3.5 %copy-start.6 = (s32[320,2]{0,1:T(2,128)S(1)}, s32[320,2]{0,1:T(2,128)}, u32[]{:S(2)}) copy-start(s32[320,2]{0,1:T(2,128)} %param.12) | copy-start | bytes 7684
  0.1 3.7 %copy-start.4 = (s32[4,4,20]{2,1,0:T(4,128)S(1)}, s32[4,4,20]{2,1,0:T(4,128)}, u32[]{:S(2)}) copy-start(s32[4,4,20]{2,1,0:T(4,128)} %param.10) | copy-start | bytes 3844
  0.1 10.2 %copy-start.3 = (bf16[30720,32]{0,1:T(8,128)(2,1)S(1)}, bf16[30720,32]{0,1:T(8,128)(2,1)}, u32[]{:S(2)}) copy-start(bf16[30720,32]{0,1:T(8,128)(2,1)} %param.9) | copy-start | bytes 5898244
  3.2 7.0 %collective-permute-start.30 = (bf16[8,4,32,480]{3,2,1,0:T(8,128)(2,1)S(1)}, bf16[8,4,32,480]{3,2,1,0:T(8,128)(2,1)}, u32[]{:S(2)}, u32[]{:S(2)}) collective-permute-start(bf16[8,4,32,480]{3,2,1,0:T(8,128)(2,1)S(1)} %get-tuple-element.160), channel_id=1, source_target_pairs={{0,4},{4,0},{1,5},{5,1},{2,6},{6,2},{3,7},{7,3},{8,12},{12,8},{9,1... | collective-permute-start | bytes 2949128 | tf_op jit(solution)/shard_map/ppermute | solution.py:260
  20.1 42.0 %all-to-all-start.1 = ((bf16[32,5,32,128]{3,2,1,0:T(8,128)(2,1)}), bf16[32,5,32,128]{3,2,1,0:T(8,128)(2,1)}, u32[]{:S(2)}, u32[]{:S(2)}) async-start(bf16[32,5,32,128]{3,2,1,0:T(8,128)(2,1)} %tile_pick.6.after), calls=%async_computation.1 | async-start | bytes 2621440 | tf_op jit(solution)/shard_map/cond/branch_0_fun/all_to_all | solution.py:330
  29.2 24.1 %collective-permute-start.3 = (bf16[8,4,32,480]{3,2,1,0:T(8,128)(2,1)S(1)}, bf16[8,4,32,480]{3,2,1,0:T(8,128)(2,1)S(1)}, u32[]{:S(2)}, u32[]{:S(2)}) collective-permute-start(bf16[8,4,32,480]{3,2,1,0:T(8,128)(2,1)S(1)} %get-tuple-element.84), channel_id=1, source_target_pairs={{0,4},{4,0},{1,5},{5,1},{2,6},{6,2},{3,7},{7,3},{8,12},{12,8},{9,1... | collective-permute-start | bytes 2949128 | tf_op jit(solution)/shard_map/cond/branch_0_fun/ppermute | solution.py:260
  30.2 12.0 %collective-permute-start = (bf16[20,32,128]{2,1,0:T(8,128)(2,1)S(1)}, bf16[20,32,128]{2,1,0:T(8,128)(2,1)S(1)}, u32[]{:S(2)}, u32[]{:S(2)}) collective-permute-start(bf16[20,32,128]{2,1,0:T(8,128)(2,1)S(1)} %get-tuple-element.78), channel_id=1, source_target_pairs={{0,1},{1,2},{2,3},{3,0},{4,5},{5,6},{6,7},{7,4},{8,9},{9,10},{10,1... | collective-permute-start | bytes 491528 | tf_op jit(solution)/shard_map/cond/branch_0_fun/ppermute | solution.py:322
  35.9 11.0 %collective-permute-start.1 = (bf16[20,32,128]{2,1,0:T(8,128)(2,1)S(1)}, bf16[20,32,128]{2,1,0:T(8,128)(2,1)S(1)}, u32[]{:S(2)}, u32[]{:S(2)}) collective-permute-start(bf16[20,32,128]{2,1,0:T(8,128)(2,1)S(1)} %get-tuple-element.79), channel_id=1, source_target_pairs={{0,2},{1,3},{2,0},{3,1},{4,6},{5,7},{6,4},{7,5},{8,10},{9,11},{10,... | collective-permute-start | bytes 491528 | tf_op jit(solution)/shard_map/cond/branch_0_fun/ppermute | solution.py:322
  38.8 8.1 %collective-permute-start.2 = (bf16[20,32,128]{2,1,0:T(8,128)(2,1)S(1)}, bf16[20,32,128]{2,1,0:T(8,128)(2,1)S(1)}, u32[]{:S(2)}, u32[]{:S(2)}) collective-permute-start(bf16[20,32,128]{2,1,0:T(8,128)(2,1)S(1)} %get-tuple-element.80), channel_id=1, source_target_pairs={{0,3},{1,0},{2,1},{3,2},{4,7},{5,4},{6,5},{7,6},{8,11},{9,8},{10,9... | collective-permute-start | bytes 491528 | tf_op jit(solution)/shard_map/cond/branch_0_fun/ppermute | solution.py:322
  60.9 1.1 copy-start.2
  62.0 39.8 %all-to-all-start = ((bf16[32,5,32,128]{3,2,1,0:T(8,128)(2,1)}), bf16[32,5,32,128]{3,2,1,0:T(8,128)(2,1)}, u32[]{:S(2)}, u32[]{:S(2)}) async-start(bf16[32,5,32,128]{3,2,1,0:T(8,128)(2,1)} %copy-done.2), calls=%async_computation | async-start | bytes 2621440 | tf_op jit(solution)/shard_map/cond/branch_0_fun/all_to_all | solution.py:330
  71.2 39.6 %collective-permute-start.7 = (bf16[20,32,128]{2,1,0:T(8,128)(2,1)}, bf16[20,32,128]{2,1,0:T(8,128)(2,1)S(1)}, u32[]{:S(2)}, u32[]{:S(2)}) collective-permute-start(bf16[20,32,128]{2,1,0:T(8,128)(2,1)} %get-tuple-element.90), channel_id=1, source_target_pairs={{0,1},{1,2},{2,3},{3,0},{4,5},{5,6},{6,7},{7,4},{8,9},{9,10},{10,1... | collective-permute-start | bytes 491528 | tf_op jit(solution)/shard_map/cond/branch_0_fun/ppermute | solution.py:322
  75.4 37.5 %collective-permute-start.8 = (bf16[20,32,128]{2,1,0:T(8,128)(2,1)}, bf16[20,32,128]{2,1,0:T(8,128)(2,1)S(1)}, u32[]{:S(2)}, u32[]{:S(2)}) collective-permute-start(bf16[20,32,128]{2,1,0:T(8,128)(2,1)} %get-tuple-element.91), channel_id=1, source_target_pairs={{0,2},{1,3},{2,0},{3,1},{4,6},{5,7},{6,4},{7,5},{8,10},{9,11},{10,... | collective-permute-start | bytes 491528 | tf_op jit(solution)/shard_map/cond/branch_0_fun/ppermute | solution.py:322
  78.3 34.6 %collective-permute-start.9 = (bf16[20,32,128]{2,1,0:T(8,128)(2,1)S(1)}, bf16[20,32,128]{2,1,0:T(8,128)(2,1)S(1)}, u32[]{:S(2)}, u32[]{:S(2)}) collective-permute-start(bf16[20,32,128]{2,1,0:T(8,128)(2,1)S(1)} %get-tuple-element.92), channel_id=1, source_target_pairs={{0,3},{1,0},{2,1},{3,2},{4,7},{5,4},{6,5},{7,6},{8,11},{9,8},{10,9... | collective-permute-start | bytes 491528 | tf_op jit(solution)/shard_map/cond/branch_0_fun/ppermute | solution.py:322
  103.7 12.6 %collective-permute-start.4 = (bf16[20,32,128]{2,1,0:T(8,128)(2,1)S(1)}, bf16[20,32,128]{2,1,0:T(8,128)(2,1)S(1)}, u32[]{:S(2)}, u32[]{:S(2)}) collective-permute-start(bf16[20,32,128]{2,1,0:T(8,128)(2,1)S(1)} %get-tuple-element.86), channel_id=1, source_target_pairs={{0,1},{1,2},{2,3},{3,0},{4,5},{5,6},{6,7},{7,4},{8,9},{9,10},{10,1... | collective-permute-start | bytes 491528 | tf_op jit(solution)/shard_map/cond/branch_0_fun/ppermute | solution.py:322
  107.9 9.7 %collective-permute-start.5 = (bf16[20,32,128]{2,1,0:T(8,128)(2,1)S(1)}, bf16[20,32,128]{2,1,0:T(8,128)(2,1)S(1)}, u32[]{:S(2)}, u32[]{:S(2)}) collective-permute-start(bf16[20,32,128]{2,1,0:T(8,128)(2,1)S(1)} %get-tuple-element.87), channel_id=1, source_target_pairs={{0,2},{1,3},{2,0},{3,1},{4,6},{5,7},{6,4},{7,5},{8,10},{9,11},{10,... | collective-permute-start | bytes 491528 | tf_op jit(solution)/shard_map/cond/branch_0_fun/ppermute | solution.py:322
  110.8 6.8 %collective-permute-start.6 = (bf16[20,32,128]{2,1,0:T(8,128)(2,1)S(1)}, bf16[20,32,128]{2,1,0:T(8,128)(2,1)S(1)}, u32[]{:S(2)}, u32[]{:S(2)}) collective-permute-start(bf16[20,32,128]{2,1,0:T(8,128)(2,1)S(1)} %get-tuple-element.88), channel_id=1, source_target_pairs={{0,3},{1,0},{2,1},{3,2},{4,7},{5,4},{6,5},{7,6},{8,11},{9,8},{10,9... | collective-permute-start | bytes 491528 | tf_op jit(solution)/shard_map/cond/branch_0_fun/ppermute | solution.py:322
where the time goes:
time: 123 us; the launch traced here: 121 us
  starting transfers between devices  42.8 us (35%)
  Pallas kernels  41 us (33%)
  waiting for transfers between devices  28.8 us (23%)
  other arithmetic  3.62 us (3%)
  local copies, waits for them, and re-layouts  3.07 us (2%)
  between operations  1.49 us (1%)
    ppermute x9, starting transfers between devices, exchange_owners(): lax.ppermute(sent[k], 'sp', [(i, (i + k) % groups) for i in range(groups)])  29 us
    all_to_all x2, waiting for transfers between devices, tiles(): return (picked, lax.all_to_all(picked, ('x', 'z'), 0, 0, tiled=True))  21.2 us
    pallas_call x2, Pallas kernels, tile_pick(): pl.pallas_call(tile_pick_kernel, out_shape=jax.ShapeDtypeStruct((rows, ca...  17.4 us
    all_to_all x2, starting transfers between devices, tiles(): return (picked, lax.all_to_all(picked, ('x', 'z'), 0, 0, tiled=True))  13.6 us
    ppermute x9, waiting for transfers between devices, exchange_owners(): lax.ppermute(sent[k], 'sp', [(i, (i + k) % groups) for i in range(groups)])  7.56 us
    pallas_call x2, Pallas kernels, product(): pl.pallas_call(functools.partial(product_kernel, per, groups), out_shape=...  6.65 us
    pallas_call x1, Pallas kernels, coef_join(): pl.pallas_call(coef_join_kernel, out_shape=jax.ShapeDtypeStruct((owned, B...  6.41 us
    pallas_call x2, Pallas kernels, core_split(): pl.pallas_call(functools.partial(core_split_kernel, batch), out_shape=[ja...  5.24 us
  transfers between devices with their start and end apart: 13, of which 4 were waited for; matrix products, arithmetic and copies ran while one was open for 5% of the time, Pallas kernels for 21%

commit v1 on v0

--- a/solution.py
+++ b/solution.py
@@ -115,55 +115,58 @@
     )(at, pairs)
 
 
-def cut_tile(odd, t, left, right, out, j):
-    rows, occ, width = left.shape
-    lo = t * BLK - (BLK // 2 if odd else 0)
-    first, last = max(lo, 0), min(lo + BLK, 2 * width)
-
-    def row(i, _):
-        parts = []
-        if lo < 0:
-            parts.append(jnp.zeros((occ, -lo), BF))
-        if first < width:
-            parts.append(left[i, :, first : min(last, width)])
-        if last > width:
-            parts.append(right[i, :, max(first, width) - width : last - width])
-        if last < lo + BLK:
-            parts.append(jnp.zeros((occ, lo + BLK - last), BF))
-        to = i % NX * NZ + i // NX
-        out[to, j] = parts[0] if len(parts) == 1 else jnp.concatenate(parts, axis=1)
+def tile_pick_kernel(at, listed, own, got, after, out, token):
+    rows, occ, width = own.shape
+    token[0] = at[0]
+    half = BLK // 2 * (at[0] % 2)
+    source = lax.broadcasted_iota(jnp.int32, (width, BLK), 0)
+    column = lax.broadcasted_iota(jnp.int32, (width, BLK), 1)
+    per = 8
+
+    def keep(j, _):
+        start = listed[j] * BLK - half
+        own_from, got_from = width * at[1], width * (1 - at[1])
+
+        def overlaps(base):
+            return (start < base + width) & (start + BLK > base)
+
+        def move(*parts):
+            picks = [(ref, (source == column + (start - base)).astype(BF)) for ref, base in parts]
+
+            def some(i, _):
+                total = sum(
+                    jnp.dot(
+                        ref[pl.ds(i * per, per)].reshape(per * occ, width),
+                        pick,
+                        preferred_element_type=jnp.float32,
+                    )
+                    for ref, pick in picks
+                )
+                out[pl.ds(i * per, per), j] = total.astype(BF).reshape(per, occ, BLK)
+                return 0
+
+            lax.fori_loop(0, rows // per, some, 0, unroll=1)
+
+        in_own, in_got = overlaps(own_from), overlaps(got_from)
+        pl.when(in_own & in_got)(lambda: move((own, own_from), (got, got_from)))
+        pl.when(in_own & jnp.logical_not(in_got))(lambda: move((own, own_from)))
+        pl.when(in_got & jnp.logical_not(in_own))(lambda: move((got, got_from)))
         return 0
 
-    lax.fori_loop(0, rows, row, 0)
-
-
-def tile_pick_kernel(at, listed, own, got, after, out):
     held = listed.shape[0] - 1
-    for odd in (0, 1):
-        for core in (0, 1):
-            left, right = (own, got) if core == 0 else (got, own)
-
-            @pl.when((at[0] % 2 == odd) & (at[1] == core))
-            def _():
-                def keep(j, _):
-                    for t in range(held):
-
-                        @pl.when(listed[j] == t)
-                        def _():
-                            cut_tile(odd, t, left, right, out, j)
-
-                    return 0
-
-                lax.fori_loop(0, jnp.minimum(listed[held], out.shape[1]), keep, 0)
+    lax.fori_loop(0, jnp.minimum(listed[held], out.shape[1]), keep, 0)
 
 
 def tile_pick(at, listed, own, got, after, cap):
     rows, occ, width = own.shape
     return pl.pallas_call(
         tile_pick_kernel,
-        out_shape=jax.ShapeDtypeStruct((rows, cap, occ, BLK), BF),
+        out_shape=[
+            jax.ShapeDtypeStruct((rows, cap, occ, BLK), BF),
+            jax.ShapeDtypeStruct((1,), jnp.int32),
+        ],
         in_specs=[SMEM, SMEM, VMEM, VMEM, ANY],
-        out_specs=VMEM,
+        out_specs=[VMEM, SMEM],
         compiler_params=params(16),
         cost_estimate=cost(4 << 20),
         name="tile_pick",
@@ -182,7 +185,7 @@
             out[t] = jnp.where(low, got[a >> 3, a & 7], got[b >> 3, b & 7])
             return 0
 
-        lax.fori_loop(0, slots, step, 0, unroll=5)
+        lax.fori_loop(0, slots, step, 0, unroll=4)
 
 
 def slot_pick(me, spots, got, groups):
@@ -283,19 +286,6 @@
     before = (tile_ids[None, :] < tile_ids[:, None]).astype(jnp.int32)
     rank = jnp.sum(my_need[:, None, :] * before[None], axis=2)
     my_cols = lax.dynamic_index_in_dim(col_ids, me_s, 0, keepdims=False)
-    my_rows = lax.dynamic_index_in_dim(row_ids, me_s, 0, keepdims=False)
-    my_live = lax.dynamic_index_in_dim(valid.reshape(groups, -1), me_s, 0, keepdims=False)
-    slot_cols = my_cols.reshape(groups, capacity)
-    slot_cols = jnp.where(my_live.reshape(groups, capacity), slot_cols, slot_cols[:, :1])
-    slot_cols = slot_cols.reshape(-1)
-    two_chips, within = slot_cols // pair_blocks, slot_cols % pair_blocks
-    upper = jnp.arange(2, dtype=jnp.int32)[:, None]
-    on_odd = (within[None, :] > held - 1 - upper).astype(jnp.int32)
-    chip = 2 * two_chips[None, :] + on_odd
-    tile = within[None, :] - on_odd * (pair_blocks - held)
-    tile_hit = (chip * held + tile)[:, :, None] == jnp.arange(NZ * NX * held, dtype=jnp.int32)
-    order = jnp.sum(jnp.where(tile_hit, rank.reshape(-1), 0), axis=2)
-    spots = (8 * (chip % NX * NZ + chip // NX) + order).reshape(-1)
     my_chip = me_z * NX + lax.axis_index("x")
     chip_need = lax.dynamic_index_in_dim(my_need, my_chip, 0, keepdims=False)
     chip_rank = lax.dynamic_index_in_dim(rank, my_chip, 0, keepdims=False)
@@ -308,41 +298,61 @@
         axis=1,
     )
     listed = jnp.concatenate([listed, jnp.sum(chip_need, keepdims=True)])
-    to_me = lax.dynamic_index_in_dim(lists, me_s, 1, keepdims=False)
-    to_me_valid = lax.dynamic_index_in_dim(valid, me_s, 1, keepdims=False)
-    hits = (to_me[:, None, :] == jnp.arange(owned, dtype=jnp.int32)[None, :, None]) & to_me_valid[
-        :, None, :
-    ]
-    slot_no = jnp.arange(capacity, dtype=jnp.int32) + 1
-    pos = (jnp.sum(jnp.where(hits, slot_no, 0), axis=2) - 1).reshape(-1)
-
-    me = me_s[None].astype(jnp.int32)
+    me = jnp.stack([me_s, me_z]).astype(jnp.int32)
+
     def exchange_owners(sent):
         return [sent[0]] + [
             lax.ppermute(sent[k], "sp", [(i, (i + k) % groups) for i in range(groups)])
             for k in range(1, groups)
         ]
 
-    def finish(cap, halves0, pairs, coef_t, my_rows, pos, listed, spots):
+    def tables(lists, valid, row_ids, my_cols, rank):
+        my_live = lax.dynamic_index_in_dim(valid.reshape(groups, -1), me_s, 0, keepdims=False)
+        my_rows = lax.dynamic_index_in_dim(row_ids, me_s, 0, keepdims=False)
+        slot_cols = my_cols.reshape(groups, capacity)
+        slot_cols = jnp.where(my_live.reshape(groups, capacity), slot_cols, slot_cols[:, :1])
+        slot_cols = slot_cols.reshape(-1)
+        two_chips, within = slot_cols // pair_blocks, slot_cols % pair_blocks
+        upper = jnp.arange(2, dtype=jnp.int32)[:, None]
+        on_odd = (within[None, :] > held - 1 - upper).astype(jnp.int32)
+        chip = 2 * two_chips[None, :] + on_odd
+        tile = within[None, :] - on_odd * (pair_blocks - held)
+        tile_hit = (chip * held + tile)[:, :, None] == jnp.arange(NZ * NX * held, dtype=jnp.int32)
+        order = jnp.sum(jnp.where(tile_hit, rank.reshape(-1), 0), axis=2)
+        spots = (8 * chip + order).reshape(-1)
+        to_me = lax.dynamic_index_in_dim(lists, me_s, 1, keepdims=False)
+        to_me_valid = lax.dynamic_index_in_dim(valid, me_s, 1, keepdims=False)
+        hits = (to_me[:, None, :] == jnp.arange(owned, dtype=jnp.int32)[None, :, None]) & to_me_valid[
+            :, None, :
+        ]
+        slot_no = jnp.arange(capacity, dtype=jnp.int32) + 1
+        pos = (jnp.sum(jnp.where(hits, slot_no, 0), axis=2) - 1).reshape(-1)
+
+        return my_rows, pos, spots
+
+    def finish(cap, halves0, pairs, coef_t, listed, *lookups):
         def tiles(halves, after):
             halves = [half.reshape(NZ * NX, occ, width) for half in halves]
-            picked = tile_pick(at, listed, *halves, after, cap)
-            return picked, lax.all_to_all(picked, ("x", "z"), 0, 0, tiled=True)
+            picked, token = tile_pick(at, listed, *halves, after, cap)
+            return token, lax.all_to_all(picked, ("z", "x"), 0, 0, tiled=True)
 
         def owners(got):
             return exchange_owners(slot_pick(me, spots, got, groups))
 
-        picked0, got0 = tiles(halves0, me)
-        coef_parts = exchange_owners(coef_pick(me, coef_t, my_rows, picked0, groups))
+        token, got0 = tiles(halves0, me)
+        *lookups, token = lax.optimization_barrier((*lookups, token))
+        my_rows, pos, spots = tables(*lookups)
+        coef_parts = exchange_owners(coef_pick(me, coef_t, my_rows, token, groups))
         coef = coef_join(me, coef_parts, pos, owned)
         _, got1 = tiles(swap(core_split(1, at, pairs)), coef)
         out = product(0, batches, me, coef, owners(got0), pos, None)
         return product(1, batches, me, coef, owners(got1), pos, out)
 
     level = sum((most > cap).astype(jnp.int32) for cap in LEVELS[:-1])
-    level, *tables = lax.optimization_barrier((level, my_rows, pos, listed, spots))
+    level, listed = lax.optimization_barrier((level, listed))
+    lookups = (lists, valid, row_ids, my_cols, rank)
     branches = [functools.partial(finish, cap) for cap in LEVELS]
-    return lax.switch(level, branches, halves0, pairs, occ_coef.T, *tables)
+    return lax.switch(level, branches, halves0, pairs, occ_coef.T, listed, *lookups)
 
 
 def solution(mesh):

time: 123 us -> 116 us (0.943)
  the two profiles are of different devices: /device:TPU:34 before, /device:TPU:4 now
where the time goes in v1:
time: 116 us; the launch traced here: 114 us
  waiting for transfers between devices  39.5 us (34%)
  starting transfers between devices  34.4 us (30%)
  Pallas kernels  29.4 us (25%)
  local copies, waits for them, and re-layouts  5.14 us (4%)
  other arithmetic  3.86 us (3%)
  between operations  1.44 us (1%)
    all_to_all x2, waiting for transfers between devices, tiles(): return (token, lax.all_to_all(picked, ('z', 'x'), 0, 0, tiled=True))  30.5 us
    all_to_all x2, starting transfers between devices, tiles(): return (token, lax.all_to_all(picked, ('z', 'x'), 0, 0, tiled=True))  20.7 us
    ppermute x9, starting transfers between devices, exchange_owners(): lax.ppermute(sent[k], 'sp', [(i, (i + k) % groups) for i in range(groups)])  13.6 us
    ppermute x9, waiting for transfers between devices, exchange_owners(): lax.ppermute(sent[k], 'sp', [(i, (i + k) % groups) for i in range(groups)])  8.95 us
    pallas_call x2, Pallas kernels, product(): pl.pallas_call(functools.partial(product_kernel, per, groups), out_shape=...  6.68 us
    pallas_call x1, Pallas kernels, coef_join(): pl.pallas_call(coef_join_kernel, out_shape=jax.ShapeDtypeStruct((owned, B...  6.42 us
    pallas_call x2, Pallas kernels, core_split(): pl.pallas_call(functools.partial(core_split_kernel, batch), out_shape=[ja...  5.23 us
    pallas_call x2, Pallas kernels, tile_pick(): pl.pallas_call(tile_pick_kernel, out_shape=[jax.ShapeDtypeStruct((rows, c...  5.23 us
  transfers between devices with their start and end apart: 13, of which 6 were waited for; matrix products, arithmetic and copies ran while one was open for 5% of the time, Pallas kernels for 19%

profile of v1, /device:TPU:4, one launch (start us, length us, event | category | flops | bytes accessed | tf_op | source)
XLA Modules:
  0.0 114.0 jit_solution(536054309854818356)
XLA Ops:
  0.1 2.1 %core_split0.1 = (bf16[8,4,32,480]{3,2,1,0:T(8,128)(2,1)S(1)}, bf16[8,4,32,480]{3,2,1,0:T(8,128)(2,1)S(1)}) custom-call(s32[2]{0:T(128)S(1)} %pad_add_fusion.1.at, bf16[2,8,4,2,32,480]{5,4,3,2,1,0:T(8,128)(2,1)} %bitcast.56), custom_call_target="tpu_custom_call" | custom-call | bytes 4194304 | tf_op jit(solution)/shard_map/core_split0/pallas_call | solution.py:106
  7.7 106.3 %conditional.1 = (bf16[2,1,80,128,128]{4,3,2,1,0:T(8,128)(2,1)}) conditional(s32[]{:T(128)} %clamp.10, (bf16[8,4,32,480]{3,2,1,0:T(8,128)(2,1)S(1)}, bf16[8,4,32,480]{3,2,1,0:T(8,128)(2,1)S(1)}, s32[2]{0:T(128)S(1)}, s32[9]{0:T(128)S(1)}, s32[2]{0:T(128)S(1)}, /*index=5*/s32[4,4,20]{2,0,1:T(4,128)S(1)}, ...), branch_computations={%region_8.11_spmd, %region_11.14_spmd, %region_14.17_spmd} | conditional | flops 671444992 | bytes 84824976 | solution.py:355
  7.7 2.5 %tile_pick.6 = (bf16[32,5,32,128]{3,2,1,0:T(8,128)(2,1)}, s32[1]{0:T(128)}) custom-call(s32[2]{0:T(128)S(1)} %get-tuple-element.93.at, s32[9]{0:T(128)S(1)} %get-tuple-element.94.listed, bf16[32,32,480]{2,1,0:T(8,128)(2,1)S(1)} %bitcast.63, bf16[32,32,480]{2,1,0:T(8,128)(2,1)S(1)} %bitcast.66, s32[2]{0:T(128)S(1)} %get-tuple-element.86.after.me), custom_call_target="tpu_custom_call" | custom-call | bytes 4194304 | tf_op jit(solution)/shard_map/cond/branch_0_fun/tile_pick/pallas_call | solution.py:162
  10.3 14.0 %all-to-all-start.1 = ((bf16[32,5,32,128]{3,2,1,0:T(8,128)(2,1)}), bf16[32,5,32,128]{3,2,1,0:T(8,128)(2,1)}, u32[]{:S(2)}, u32[]{:S(2)}) async-start(bf16[32,5,32,128]{3,2,1,0:T(8,128)(2,1)} %get-tuple-element.118), calls=%async_computation.1 | async-start | bytes 2621440 | tf_op jit(solution)/shard_map/cond/branch_0_fun/all_to_all | solution.py:337
  24.3 3.1 %core_split1.3 = (bf16[8,4,32,480]{3,2,1,0:T(8,128)(2,1)S(1)}, bf16[8,4,32,480]{3,2,1,0:T(8,128)(2,1)}) custom-call(s32[2]{0:T(128)S(1)} %get-tuple-element.93.at, bf16[2,8,4,2,32,480]{5,4,3,2,1,0:T(8,128)(2,1)} %get-tuple-element.110.pairs), custom_call_target="tpu_custom_call" | custom-call | bytes 4194304 | tf_op jit(solution)/shard_map/cond/branch_0_fun/core_split1/pallas_call | solution.py:106
  28.7 1.4 %coef_pick.3 = (bf16[20,32,128]{2,1,0:T(8,128)(2,1)S(1)}, bf16[20,32,128]{2,1,0:T(8,128)(2,1)S(1)}, bf16[20,32,128]{2,1,0:T(8,128)(2,1)S(1)}, bf16[20,32,128]{2,1,0:T(8,128)(2,1)S(1)}) custom-call(s32[2]{0:T(128)S(1)} %get-tuple-element.86.after.me, s32[80]{0:T(128)S(1)} %fusion.6.rows, bf16[32,30720]{1,0:T(8,128)(2,1)S(1)} %copy-done.9, ...), custom_call_target="tpu_custom_call" | custom-call | bytes 4194304 | tf_op jit(solution)/shard_map/cond/branch_0_fun/coef_pick/pallas_call | solution.py:48
  30.2 2.9 %collective-permute-start.1 = (bf16[20,32,128]{2,1,0:T(8,128)(2,1)S(1)}, bf16[20,32,128]{2,1,0:T(8,128)(2,1)S(1)}, u32[]{:S(2)}, u32[]{:S(2)}) collective-permute-start(bf16[20,32,128]{2,1,0:T(8,128)(2,1)S(1)} %get-tuple-element.106), channel_id=1, source_target_pairs={{0,2},{1,3},{2,0},{3,1},{4,6},{5,7},{6,4},{7,5},{8,10},{9,11},{10,... | collective-permute-start | bytes 491528 | tf_op jit(solution)/shard_map/cond/branch_0_fun/ppermute | solution.py:305
  33.1 1.8 %collective-permute-start.2 = (bf16[20,32,128]{2,1,0:T(8,128)(2,1)S(1)}, bf16[20,32,128]{2,1,0:T(8,128)(2,1)S(1)}, u32[]{:S(2)}, u32[]{:S(2)}) collective-permute-start(bf16[20,32,128]{2,1,0:T(8,128)(2,1)S(1)} %get-tuple-element.107), channel_id=1, source_target_pairs={{0,3},{1,0},{2,1},{3,2},{4,7},{5,4},{6,5},{7,6},{8,11},{9,8},{10,9... | collective-permute-start | bytes 491528 | tf_op jit(solution)/shard_map/cond/branch_0_fun/ppermute | solution.py:305
  35.4 6.2 %collective-permute-done.rest_1_ = bf16[20,32,128]{2,1,0:T(8,128)(2,1)S(1)} collective-permute-done((bf16[20,32,128]{2,1,0:T(8,128)(2,1)S(1)}, bf16[20,32,128]{2,1,0:T(8,128)(2,1)S(1)}, u32[]{:S(2)}, u32[]{:S(2)}) %collective-permute-start) | collective-permute-done | bytes 163872 | tf_op jit(solution)/shard_map/cond/branch_0_fun/ppermute | solution.py:305
  42.2 6.4 %coef_join.3.after.coef = bf16[80,128,128]{2,1,0:T(8,128)(2,1)S(1)} custom-call(s32[2]{0:T(128)S(1)} %get-tuple-element.86.after.me, s32[320]{0:T(512)S(1)} %sub.69.pos, bf16[20,32,128]{2,1,0:T(8,128)(2,1)S(1)} %get-tuple-element.104.rest_0_, bf16[20,32,128]{2,1,0:T(8,128)(2,1)S(1)} %collective-permute-done.rest_1_, ...), custom_call_target="tpu_custom_call" | custom-call | bytes 4194304 | tf_op jit(solution)/shard_map/cond/branch_0_fun/coef_join/pallas_call | solution.py:80
  48.6 1.2 %copy-done.4 = bf16[8,4,32,480]{3,2,1,0:T(8,128)(2,1)S(1)} copy-done((bf16[8,4,32,480]{3,2,1,0:T(8,128)(2,1)S(1)}, bf16[8,4,32,480]{3,2,1,0:T(8,128)(2,1)}, u32[]{:S(2)}) %copy-start.4) | copy-done | bytes 983064 | tf_op jit(solution)/shard_map/cond
  49.8 2.7 %tile_pick.7 = (bf16[32,5,32,128]{3,2,1,0:T(8,128)(2,1)S(1)}, s32[1]{0:T(128)}) custom-call(s32[2]{0:T(128)S(1)} %get-tuple-element.93.at, s32[9]{0:T(128)S(1)} %get-tuple-element.94.listed, bf16[32,32,480]{2,1,0:T(8,128)(2,1)S(1)} %bitcast.53, bf16[32,32,480]{2,1,0:T(8,128)(2,1)} %bitcast.8.got, bf16[80,128,128]{2,1,0:T(8,128)(2,1)S(1)} %coef_join.3.after.coef), custom_call_target="tpu_custom_call" | custom-call | bytes 4194304 | tf_op jit(solution)/shard_map/cond/branch_0_fun/tile_pick/pallas_call | solution.py:162
  53.6 5.1 %all-to-all-done.1.got = bf16[32,5,32,128]{3,2,1,0:T(8,128)(2,1)} async-done(((bf16[32,5,32,128]{3,2,1,0:T(8,128)(2,1)}), bf16[32,5,32,128]{3,2,1,0:T(8,128)(2,1)}, u32[]{:S(2)}, u32[]{:S(2)}) %all-to-all-start.1) | async-done | bytes 1310752 | tf_op jit(solution)/shard_map/cond/branch_0_fun/all_to_all | solution.py:337
  58.7 6.7 %all-to-all-start = ((bf16[32,5,32,128]{3,2,1,0:T(8,128)(2,1)}), bf16[32,5,32,128]{3,2,1,0:T(8,128)(2,1)}, u32[]{:S(2)}, u32[]{:S(2)}) async-start(bf16[32,5,32,128]{3,2,1,0:T(8,128)(2,1)} %copy-done.2), calls=%async_computation | async-start | bytes 2621440 | tf_op jit(solution)/shard_map/cond/branch_0_fun/all_to_all | solution.py:337
  66.3 2.6 %slot_pick.7 = (bf16[20,32,128]{2,1,0:T(8,128)(2,1)S(1)}, bf16[20,32,128]{2,1,0:T(8,128)(2,1)}, bf16[20,32,128]{2,1,0:T(8,128)(2,1)}, bf16[20,32,128]{2,1,0:T(8,128)(2,1)S(1)}) custom-call(s32[2]{0:T(128)S(1)} %get-tuple-element.86.after.me, s32[160]{0:T(256)S(1)} %reshape.375.spots, bf16[32,5,32,128]{3,2,1,0:T(8,128)(2,1)} %all-to-all-done.1.got), custom_call_target="tpu_custom_call" | custom-call | bytes 2097152 | tf_op jit(solution)/shard_map/cond/branch_0_fun/slot_pick/pallas_call | solution.py:194
  68.9 2.5 %collective-permute-start.8 = (bf16[20,32,128]{2,1,0:T(8,128)(2,1)}, bf16[20,32,128]{2,1,0:T(8,128)(2,1)S(1)}, u32[]{:S(2)}, u32[]{:S(2)}) collective-permute-start(bf16[20,32,128]{2,1,0:T(8,128)(2,1)} %get-tuple-element.121), channel_id=1, source_target_pairs={{0,2},{1,3},{2,0},{3,1},{4,6},{5,7},{6,4},{7,5},{8,10},{9,11},{10,... | collective-permute-start | bytes 491528 | tf_op jit(solution)/shard_map/cond/branch_0_fun/ppermute | solution.py:305
  71.5 1.9 %collective-permute-start.9 = (bf16[20,32,128]{2,1,0:T(8,128)(2,1)S(1)}, bf16[20,32,128]{2,1,0:T(8,128)(2,1)S(1)}, u32[]{:S(2)}, u32[]{:S(2)}) collective-permute-start(bf16[20,32,128]{2,1,0:T(8,128)(2,1)S(1)} %get-tuple-element.122), channel_id=1, source_target_pairs={{0,3},{1,0},{2,1},{3,2},{4,7},{5,4},{6,5},{7,6},{8,11},{9,8},{10,9... | collective-permute-start | bytes 491528 | tf_op jit(solution)/shard_map/cond/branch_0_fun/ppermute | solution.py:305
  73.3 25.4 %all-to-all-done.got = bf16[32,5,32,128]{3,2,1,0:T(8,128)(2,1)} async-done(((bf16[32,5,32,128]{3,2,1,0:T(8,128)(2,1)}), bf16[32,5,32,128]{3,2,1,0:T(8,128)(2,1)}, u32[]{:S(2)}, u32[]{:S(2)}) %all-to-all-start) | async-done | bytes 1310752 | tf_op jit(solution)/shard_map/cond/branch_0_fun/all_to_all | solution.py:337
  98.8 1.9 %slot_pick.6 = (bf16[20,32,128]{2,1,0:T(8,128)(2,1)S(1)}, bf16[20,32,128]{2,1,0:T(8,128)(2,1)S(1)}, bf16[20,32,128]{2,1,0:T(8,128)(2,1)S(1)}, bf16[20,32,128]{2,1,0:T(8,128)(2,1)S(1)}) custom-call(s32[2]{0:T(128)S(1)} %get-tuple-element.86.after.me, s32[160]{0:T(256)S(1)} %reshape.375.spots, bf16[32,5,32,128]{3,2,1,0:T(8,128)(2,1)} %all-to-all-done.got), custom_call_target="tpu_custom_call" | custom-call | bytes 2097152 | tf_op jit(solution)/shard_map/cond/branch_0_fun/slot_pick/pallas_call | solution.py:194
  101.2 2.7 %collective-permute-start.5 = (bf16[20,32,128]{2,1,0:T(8,128)(2,1)S(1)}, bf16[20,32,128]{2,1,0:T(8,128)(2,1)S(1)}, u32[]{:S(2)}, u32[]{:S(2)}) collective-permute-start(bf16[20,32,128]{2,1,0:T(8,128)(2,1)S(1)} %get-tuple-element.116), channel_id=1, source_target_pairs={{0,2},{1,3},{2,0},{3,1},{4,6},{5,7},{6,4},{7,5},{8,10},{9,11},{10,... | collective-permute-start | bytes 491528 | tf_op jit(solution)/shard_map/cond/branch_0_fun/ppermute | solution.py:305
  103.9 1.3 %collective-permute-start.6 = (bf16[20,32,128]{2,1,0:T(8,128)(2,1)S(1)}, bf16[20,32,128]{2,1,0:T(8,128)(2,1)S(1)}, u32[]{:S(2)}, u32[]{:S(2)}) collective-permute-start(bf16[20,32,128]{2,1,0:T(8,128)(2,1)S(1)} %get-tuple-element.117), channel_id=1, source_target_pairs={{0,3},{1,0},{2,1},{3,2},{4,7},{5,4},{6,5},{7,6},{8,11},{9,8},{10,9... | collective-permute-start | bytes 491528 | tf_op jit(solution)/shard_map/cond/branch_0_fun/ppermute | solution.py:305
  105.1 3.3 %product0.3.rest_4_ = bf16[2,1,80,128,128]{4,3,2,1,0:T(8,128)(2,1)} custom-call(s32[2]{0:T(128)S(1)} %get-tuple-element.86.after.me, s32[320]{0:T(512)S(1)} %sub.69.pos, bf16[80,128,128]{2,1,0:T(8,128)(2,1)S(1)} %coef_join.3.after.coef, bf16[20,32,128]{2,1,0:T(8,128)(2,1)S(1)} %get-tuple-element.119.rest_0_, ...), custom_call_target="tpu_custom_call" | custom-call | flops 335544320 | bytes 6291456 | tf_op jit(solution)/shard_map/cond/branch_0_fun/product0/pallas_call | solution.py:227
  108.9 1.7 %collective-permute-done.5.rest_2_ = bf16[20,32,128]{2,1,0:T(8,128)(2,1)S(1)} collective-permute-done((bf16[20,32,128]{2,1,0:T(8,128)(2,1)S(1)}, bf16[20,32,128]{2,1,0:T(8,128)(2,1)S(1)}, u32[]{:S(2)}, u32[]{:S(2)}) %collective-permute-start.5) | collective-permute-done | bytes 163872 | tf_op jit(solution)/shard_map/cond/branch_0_fun/ppermute | solution.py:305
  110.6 3.3 %product1.3 = bf16[2,1,80,128,128]{4,3,2,1,0:T(8,128)(2,1)} custom-call(s32[2]{0:T(128)S(1)} %get-tuple-element.86.after.me, s32[320]{0:T(512)S(1)} %sub.69.pos, bf16[80,128,128]{2,1,0:T(8,128)(2,1)S(1)} %coef_join.3.after.coef, bf16[20,32,128]{2,1,0:T(8,128)(2,1)S(1)} %get-tuple-element.114.rest_0_, ...), custom_call_target="tpu_custom_call", output_to_operand_aliasing={{}: (7, {})} | custom-call | flops 335544320 | bytes 6291456 | tf_op jit(solution)/shard_map/cond/branch_0_fun/product1/pallas_call | solution.py:227
  (86 shorter events, 9.6 us)
Async XLA Ops:
  0.1 2.3 %copy-start.12 = (s32[320,2]{0,1:T(2,128)S(1)}, s32[320,2]{0,1:T(2,128)}, u32[]{:S(2)}) copy-start(s32[320,2]{0,1:T(2,128)} %param.12) | copy-start | bytes 7684
  0.1 2.4 %copy-start.14 = (s32[4,4]{1,0:T(4,128)S(1)}, s32[4,4]{1,0:T(4,128)}, u32[]{:S(2)}) copy-start(s32[4,4]{1,0:T(4,128)} %param.11) | copy-start | bytes 196
  0.1 2.5 %copy-start.13 = (s32[4,4,20]{2,1,0:T(4,128)S(1)}, s32[4,4,20]{2,1,0:T(4,128)}, u32[]{:S(2)}) copy-start(s32[4,4,20]{2,1,0:T(4,128)} %param.10) | copy-start | bytes 3844
  2.2 5.4 %collective-permute-start.30 = (bf16[8,4,32,480]{3,2,1,0:T(8,128)(2,1)S(1)}, bf16[8,4,32,480]{3,2,1,0:T(8,128)(2,1)S(1)}, u32[]{:S(2)}, u32[]{:S(2)}) collective-permute-start(bf16[8,4,32,480]{3,2,1,0:T(8,128)(2,1)S(1)} %get-tuple-element.211), channel_id=1, source_target_pairs={{0,4},{4,0},{1,5},{5,1},{2,6},{6,2},{3,7},{7,3},{8,12},{12,8},{9,1... | collective-permute-start | bytes 2949128 | tf_op jit(solution)/shard_map/ppermute | solution.py:263
  10.3 48.4 %all-to-all-start.1 = ((bf16[32,5,32,128]{3,2,1,0:T(8,128)(2,1)}), bf16[32,5,32,128]{3,2,1,0:T(8,128)(2,1)}, u32[]{:S(2)}, u32[]{:S(2)}) async-start(bf16[32,5,32,128]{3,2,1,0:T(8,128)(2,1)} %get-tuple-element.118), calls=%async_computation.1 | async-start | bytes 2621440 | tf_op jit(solution)/shard_map/cond/branch_0_fun/all_to_all | solution.py:337
  24.3 4.4 %copy-start.9 = (bf16[32,30720]{1,0:T(8,128)(2,1)S(1)}, bf16[32,30720]{1,0:T(8,128)(2,1)}, u32[]{:S(2)}) copy-start(bf16[32,30720]{1,0:T(8,128)(2,1)} %get-tuple-element.102.coef) | copy-start | bytes 5898244 | tf_op jit(solution)/shard_map/cond
  27.4 1.0 copy-start.3
  28.4 20.2 %collective-permute-start.3 = (bf16[8,4,32,480]{3,2,1,0:T(8,128)(2,1)}, bf16[8,4,32,480]{3,2,1,0:T(8,128)(2,1)}, u32[]{:S(2)}, u32[]{:S(2)}) collective-permute-start(bf16[8,4,32,480]{3,2,1,0:T(8,128)(2,1)} %get-tuple-element.112), channel_id=1, source_target_pairs={{0,4},{4,0},{1,5},{5,1},{2,6},{6,2},{3,7},{7,3},{8,12},{12,8},{9,1... | collective-permute-start | bytes 2949128 | tf_op jit(solution)/shard_map/cond/branch_0_fun/ppermute | solution.py:263
  30.1 11.4 %collective-permute-start = (bf16[20,32,128]{2,1,0:T(8,128)(2,1)S(1)}, bf16[20,32,128]{2,1,0:T(8,128)(2,1)S(1)}, u32[]{:S(2)}, u32[]{:S(2)}) collective-permute-start(bf16[20,32,128]{2,1,0:T(8,128)(2,1)S(1)} %get-tuple-element.105), channel_id=1, source_target_pairs={{0,1},{1,2},{2,3},{3,0},{4,5},{5,6},{6,7},{7,4},{8,9},{9,10},{10,1... | collective-permute-start | bytes 491528 | tf_op jit(solution)/shard_map/cond/branch_0_fun/ppermute | solution.py:305
  30.2 11.3 %collective-permute-start.1 = (bf16[20,32,128]{2,1,0:T(8,128)(2,1)S(1)}, bf16[20,32,128]{2,1,0:T(8,128)(2,1)S(1)}, u32[]{:S(2)}, u32[]{:S(2)}) collective-permute-start(bf16[20,32,128]{2,1,0:T(8,128)(2,1)S(1)} %get-tuple-element.106), channel_id=1, source_target_pairs={{0,2},{1,3},{2,0},{3,1},{4,6},{5,7},{6,4},{7,5},{8,10},{9,11},{10,... | collective-permute-start | bytes 491528 | tf_op jit(solution)/shard_map/cond/branch_0_fun/ppermute | solution.py:305
  33.1 9.1 %collective-permute-start.2 = (bf16[20,32,128]{2,1,0:T(8,128)(2,1)S(1)}, bf16[20,32,128]{2,1,0:T(8,128)(2,1)S(1)}, u32[]{:S(2)}, u32[]{:S(2)}) collective-permute-start(bf16[20,32,128]{2,1,0:T(8,128)(2,1)S(1)} %get-tuple-element.107), channel_id=1, source_target_pairs={{0,3},{1,0},{2,1},{3,2},{4,7},{5,4},{6,5},{7,6},{8,11},{9,8},{10,9... | collective-permute-start | bytes 491528 | tf_op jit(solution)/shard_map/cond/branch_0_fun/ppermute | solution.py:305
  48.6 1.2 %copy-start.4 = (bf16[8,4,32,480]{3,2,1,0:T(8,128)(2,1)S(1)}, bf16[8,4,32,480]{3,2,1,0:T(8,128)(2,1)}, u32[]{:S(2)}) copy-start(bf16[8,4,32,480]{3,2,1,0:T(8,128)(2,1)} %copy-done.3) | copy-start | bytes 2949124 | tf_op jit(solution)/shard_map/cond
  52.5 1.1 copy-start.2
  58.7 40.1 %all-to-all-start = ((bf16[32,5,32,128]{3,2,1,0:T(8,128)(2,1)}), bf16[32,5,32,128]{3,2,1,0:T(8,128)(2,1)}, u32[]{:S(2)}, u32[]{:S(2)}) async-start(bf16[32,5,32,128]{3,2,1,0:T(8,128)(2,1)} %copy-done.2), calls=%async_computation | async-start | bytes 2621440 | tf_op jit(solution)/shard_map/cond/branch_0_fun/all_to_all | solution.py:337
  68.9 34.9 %collective-permute-start.7 = (bf16[20,32,128]{2,1,0:T(8,128)(2,1)}, bf16[20,32,128]{2,1,0:T(8,128)(2,1)S(1)}, u32[]{:S(2)}, u32[]{:S(2)}) collective-permute-start(bf16[20,32,128]{2,1,0:T(8,128)(2,1)} %get-tuple-element.120), channel_id=1, source_target_pairs={{0,1},{1,2},{2,3},{3,0},{4,5},{5,6},{6,7},{7,4},{8,9},{9,10},{10,1... | collective-permute-start | bytes 491528 | tf_op jit(solution)/shard_map/cond/branch_0_fun/ppermute | solution.py:305
  68.9 36.2 %collective-permute-start.8 = (bf16[20,32,128]{2,1,0:T(8,128)(2,1)}, bf16[20,32,128]{2,1,0:T(8,128)(2,1)S(1)}, u32[]{:S(2)}, u32[]{:S(2)}) collective-permute-start(bf16[20,32,128]{2,1,0:T(8,128)(2,1)} %get-tuple-element.121), channel_id=1, source_target_pairs={{0,2},{1,3},{2,0},{3,1},{4,6},{5,7},{6,4},{7,5},{8,10},{9,11},{10,... | collective-permute-start | bytes 491528 | tf_op jit(solution)/shard_map/cond/branch_0_fun/ppermute | solution.py:305
  71.5 33.7 %collective-permute-start.9 = (bf16[20,32,128]{2,1,0:T(8,128)(2,1)S(1)}, bf16[20,32,128]{2,1,0:T(8,128)(2,1)S(1)}, u32[]{:S(2)}, u32[]{:S(2)}) collective-permute-start(bf16[20,32,128]{2,1,0:T(8,128)(2,1)S(1)} %get-tuple-element.122), channel_id=1, source_target_pairs={{0,3},{1,0},{2,1},{3,2},{4,7},{5,4},{6,5},{7,6},{8,11},{9,8},{10,9... | collective-permute-start | bytes 491528 | tf_op jit(solution)/shard_map/cond/branch_0_fun/ppermute | solution.py:305
  100.6 8.3 %collective-permute-start.4 = (bf16[20,32,128]{2,1,0:T(8,128)(2,1)S(1)}, bf16[20,32,128]{2,1,0:T(8,128)(2,1)S(1)}, u32[]{:S(2)}, u32[]{:S(2)}) collective-permute-start(bf16[20,32,128]{2,1,0:T(8,128)(2,1)S(1)} %get-tuple-element.115), channel_id=1, source_target_pairs={{0,1},{1,2},{2,3},{3,0},{4,5},{5,6},{6,7},{7,4},{8,9},{9,10},{10,1... | collective-permute-start | bytes 491528 | tf_op jit(solution)/shard_map/cond/branch_0_fun/ppermute | solution.py:305
  101.2 9.4 %collective-permute-start.5 = (bf16[20,32,128]{2,1,0:T(8,128)(2,1)S(1)}, bf16[20,32,128]{2,1,0:T(8,128)(2,1)S(1)}, u32[]{:S(2)}, u32[]{:S(2)}) collective-permute-start(bf16[20,32,128]{2,1,0:T(8,128)(2,1)S(1)} %get-tuple-element.116), channel_id=1, source_target_pairs={{0,2},{1,3},{2,0},{3,1},{4,6},{5,7},{6,4},{7,5},{8,10},{9,11},{10,... | collective-permute-start | bytes 491528 | tf_op jit(solution)/shard_map/cond/branch_0_fun/ppermute | solution.py:305
  103.9 6.8 %collective-permute-start.6 = (bf16[20,32,128]{2,1,0:T(8,128)(2,1)S(1)}, bf16[20,32,128]{2,1,0:T(8,128)(2,1)S(1)}, u32[]{:S(2)}, u32[]{:S(2)}) collective-permute-start(bf16[20,32,128]{2,1,0:T(8,128)(2,1)S(1)} %get-tuple-element.117), channel_id=1, source_target_pairs={{0,3},{1,0},{2,1},{3,2},{4,7},{5,4},{6,5},{7,6},{8,11},{9,8},{10,9... | collective-permute-start | bytes 491528 | tf_op jit(solution)/shard_map/cond/branch_0_fun/ppermute | solution.py:305

commit v2 on v1

--- a/solution.py
+++ b/solution.py
@@ -173,7 +173,7 @@
     )(at, listed, own, got, after)
 
 
-def slot_pick_kernel(me, spots, got, *outs):
+def slot_pick_kernel(me, spots, got, after, *outs):
     slots, occ, _ = outs[0].shape
     low = lax.broadcasted_iota(jnp.int32, (occ, BLK), 1) < BLK // 2
     total = len(outs) * slots
@@ -188,22 +188,23 @@
         lax.fori_loop(0, slots, step, 0, unroll=4)
 
 
-def slot_pick(me, spots, got, groups):
+def slot_pick(me, spots, got, after, groups):
     slots = spots.shape[0] // (2 * groups)
     occ = got.shape[2]
     return pl.pallas_call(
         slot_pick_kernel,
         out_shape=[jax.ShapeDtypeStruct((slots, occ, BLK), BF)] * groups,
-        in_specs=[SMEM, SMEM, VMEM],
+        in_specs=[SMEM, SMEM, VMEM, ANY],
         out_specs=[VMEM] * groups,
         compiler_params=params(16),
         cost_estimate=cost(2 << 20),
         name="slot_pick",
-    )(me, spots, got)
+    )(me, spots, got, after)
 
 
 def product_kernel(per, groups, me, pos, coef, *rest):
-    gamma, (out, held) = rest[:groups], rest[-2:]
+    gamma, (out, token, held) = rest[:groups], rest[-3:]
+    token[0] = me[0]
     owned = pos.shape[0] // groups
     step = pl.program_id(0)
 
@@ -226,14 +227,20 @@
     extra = [] if prior is None else [prior]
     return pl.pallas_call(
         functools.partial(product_kernel, per, groups),
-        out_shape=jax.ShapeDtypeStruct((batches, 1, owned, BLK, BLK), BF),
+        out_shape=[
+            jax.ShapeDtypeStruct((batches, 1, owned, BLK, BLK), BF),
+            jax.ShapeDtypeStruct((1,), jnp.int32),
+        ],
         grid_spec=pltpu.PrefetchScalarGridSpec(
             num_scalar_prefetch=2,
             grid=(owned // per,),
             in_specs=[pl.BlockSpec((per, BLK, coef.shape[2]), lambda i, *_: (i, 0, 0))]
             + [pl.BlockSpec(gamma[0].shape, lambda i, *_: (0, 0, 0))] * groups
             + [ANY] * len(extra),
-            out_specs=pl.BlockSpec((1, 1, per, BLK, BLK), lambda i, *_: (batch, 0, i, 0, 0)),
+            out_specs=[
+                pl.BlockSpec((1, 1, per, BLK, BLK), lambda i, *_: (batch, 0, i, 0, 0)),
+                SMEM,
+            ],
             scratch_shapes=[pltpu.VMEM((groups,) + gamma[0].shape, BF)],
         ),
         input_output_aliases={3 + groups: 0} if extra else {},
@@ -336,8 +343,8 @@
             picked, token = tile_pick(at, listed, *halves, after, cap)
             return token, lax.all_to_all(picked, ("z", "x"), 0, 0, tiled=True)
 
-        def owners(got):
-            return exchange_owners(slot_pick(me, spots, got, groups))
+        def owners(got, after):
+            return exchange_owners(slot_pick(me, spots, got, after, groups))
 
         token, got0 = tiles(halves0, me)
         *lookups, token = lax.optimization_barrier((*lookups, token))
@@ -345,8 +352,9 @@
         coef_parts = exchange_owners(coef_pick(me, coef_t, my_rows, token, groups))
         coef = coef_join(me, coef_parts, pos, owned)
         _, got1 = tiles(swap(core_split(1, at, pairs)), coef)
-        out = product(0, batches, me, coef, owners(got0), pos, None)
-        return product(1, batches, me, coef, owners(got1), pos, out)
+        out, token = product(0, batches, me, coef, owners(got0, me), pos, None)
+        out, _ = product(1, batches, me, coef, owners(got1, token), pos, out)
+        return out
 
     level = sum((most > cap).astype(jnp.int32) for cap in LEVELS[:-1])
     level, listed = lax.optimization_barrier((level, listed))

time: 116 us -> 119 us (1.026); the launches traced: 114 us -> 119 us
  starting transfers between devices: 34.4 us -> 38.4 us
    all_to_all x2, waiting for transfers between devices: 30.5 us -> 17.5 us  [tiles(): return (token, lax.all_to_all(picked, ('z', 'x'), 0, 0, tiled=True))]
    ppermute x9, waiting for transfers between devices: 8.95 us -> 21.6 us  [exchange_owners(): lax.ppermute(sent[k], 'sp', [(i, (i + k) % groups) for i in range(groups)])]
    ppermute x9, starting transfers between devices: 13.6 us -> 16.9 us  [exchange_owners(): lax.ppermute(sent[k], 'sp', [(i, (i + k) % groups) for i in range(groups)])]
  transfers between devices with their start and end apart: 13 -> 13, of which waited for: 6 -> 8; matrix products, arithmetic and copies ran while one was open for 5% -> 5% of each run, Pallas kernels for 19% -> 16%
where the time goes in v2:
time: 119 us
  waiting for transfers between devices  39.2 us (33%)
  starting transfers between devices  38.4 us (32%)
  Pallas kernels  30.1 us (25%)
  local copies, waits for them, and re-layouts  5.16 us (4%)
  other arithmetic  3.87 us (3%)
  between operations  1.64 us (1%)
    ppermute x9, waiting for transfers between devices, exchange_owners(): lax.ppermute(sent[k], 'sp', [(i, (i + k) % groups) for i in range(groups)])  21.6 us
    all_to_all x2, starting transfers between devices, tiles(): return (token, lax.all_to_all(picked, ('z', 'x'), 0, 0, tiled=True))  21.4 us
    all_to_all x2, waiting for transfers between devices, tiles(): return (token, lax.all_to_all(picked, ('z', 'x'), 0, 0, tiled=True))  17.5 us
    ppermute x9, starting transfers between devices, exchange_owners(): lax.ppermute(sent[k], 'sp', [(i, (i + k) % groups) for i in range(groups)])  16.9 us
    pallas_call x2, Pallas kernels, product(): pl.pallas_call(functools.partial(product_kernel, per, groups), out_shape=...  6.69 us
    pallas_call x1, Pallas kernels, coef_join(): pl.pallas_call(coef_join_kernel, out_shape=jax.ShapeDtypeStruct((owned, B...  6.42 us
    pallas_call x2, Pallas kernels, tile_pick(): pl.pallas_call(tile_pick_kernel, out_shape=[jax.ShapeDtypeStruct((rows, c...  5.82 us
    pallas_call x2, Pallas kernels, core_split(): pl.pallas_call(functools.partial(core_split_kernel, batch), out_shape=[ja...  5.23 us
  transfers between devices with their start and end apart: 13, of which 8 were waited for; matrix products, arithmetic and copies ran while one was open for 5% of the time, Pallas kernels for 16%

profile of v2, /device:TPU:4, one launch (start us, length us, event | category | flops | bytes accessed | tf_op | source)
XLA Modules:
  0.0 118.6 jit_solution(14054526531576822743)
XLA Ops:
  0.1 2.1 %core_split0.1 = (bf16[8,4,32,480]{3,2,1,0:T(8,128)(2,1)S(1)}, bf16[8,4,32,480]{3,2,1,0:T(8,128)(2,1)S(1)}) custom-call(s32[2]{0:T(128)S(1)} %pad_add_fusion.1.at, bf16[2,8,4,2,32,480]{5,4,3,2,1,0:T(8,128)(2,1)} %bitcast.56), custom_call_target="tpu_custom_call" | custom-call | bytes 4194304 | tf_op jit(solution)/shard_map/core_split0/pallas_call | solution.py:106
  7.7 110.7 %conditional.1 = (bf16[2,1,80,128,128]{4,3,2,1,0:T(8,128)(2,1)}) conditional(s32[]{:T(128)} %clamp.10, (bf16[8,4,32,480]{3,2,1,0:T(8,128)(2,1)S(1)}, bf16[8,4,32,480]{3,2,1,0:T(8,128)(2,1)S(1)}, s32[2]{0:T(128)S(1)}, s32[9]{0:T(128)S(1)}, s32[2]{0:T(128)S(1)}, /*index=5*/s32[4,4,20]{2,0,1:T(4,128)S(1)}, ...), branch_computations={%region_8.11_spmd, %region_11.14_spmd, %region_14.17_spmd} | conditional | flops 671444992 | bytes 84824968 | solution.py:363
  7.7 2.8 %tile_pick.6 = (bf16[32,5,32,128]{3,2,1,0:T(8,128)(2,1)}, s32[1]{0:T(128)}) custom-call(s32[2]{0:T(128)S(1)} %get-tuple-element.93.at, s32[9]{0:T(128)S(1)} %get-tuple-element.94.listed, bf16[32,32,480]{2,1,0:T(8,128)(2,1)S(1)} %bitcast.63, bf16[32,32,480]{2,1,0:T(8,128)(2,1)S(1)} %bitcast.66, s32[2]{0:T(128)S(1)} %get-tuple-element.86.after.me), custom_call_target="tpu_custom_call" | custom-call | bytes 4194304 | tf_op jit(solution)/shard_map/cond/branch_0_fun/tile_pick/pallas_call | solution.py:162
  10.6 13.1 %all-to-all-start.1 = ((bf16[32,5,32,128]{3,2,1,0:T(8,128)(2,1)}), bf16[32,5,32,128]{3,2,1,0:T(8,128)(2,1)}, u32[]{:S(2)}, u32[]{:S(2)}) async-start(bf16[32,5,32,128]{3,2,1,0:T(8,128)(2,1)} %get-tuple-element.114), calls=%async_computation.1 | async-start | bytes 2621440 | tf_op jit(solution)/shard_map/cond/branch_0_fun/all_to_all | solution.py:344
  23.6 3.1 %core_split1.3 = (bf16[8,4,32,480]{3,2,1,0:T(8,128)(2,1)S(1)}, bf16[8,4,32,480]{3,2,1,0:T(8,128)(2,1)}) custom-call(s32[2]{0:T(128)S(1)} %get-tuple-element.93.at, bf16[2,8,4,2,32,480]{5,4,3,2,1,0:T(8,128)(2,1)} %get-tuple-element.110.pairs), custom_call_target="tpu_custom_call" | custom-call | bytes 4194304 | tf_op jit(solution)/shard_map/cond/branch_0_fun/core_split1/pallas_call | solution.py:106
  28.1 1.5 %coef_pick.3 = (bf16[20,32,128]{2,1,0:T(8,128)(2,1)S(1)}, bf16[20,32,128]{2,1,0:T(8,128)(2,1)S(1)}, bf16[20,32,128]{2,1,0:T(8,128)(2,1)S(1)}, bf16[20,32,128]{2,1,0:T(8,128)(2,1)S(1)}) custom-call(s32[2]{0:T(128)S(1)} %get-tuple-element.86.after.me, s32[80]{0:T(128)S(1)} %fusion.6.rows, bf16[32,30720]{1,0:T(8,128)(2,1)S(1)} %copy-done.9, ...), custom_call_target="tpu_custom_call" | custom-call | bytes 4194304 | tf_op jit(solution)/shard_map/cond/branch_0_fun/coef_pick/pallas_call | solution.py:48
  31.0 4.7 %collective-permute-start.1 = (bf16[20,32,128]{2,1,0:T(8,128)(2,1)S(1)}, bf16[20,32,128]{2,1,0:T(8,128)(2,1)S(1)}, u32[]{:S(2)}, u32[]{:S(2)}) collective-permute-start(bf16[20,32,128]{2,1,0:T(8,128)(2,1)S(1)} %get-tuple-element.106), channel_id=1, source_target_pairs={{0,2},{1,3},{2,0},{3,1},{4,6},{5,7},{6,4},{7,5},{8,10},{9,11},{10,... | collective-permute-start | bytes 491528 | tf_op jit(solution)/shard_map/cond/branch_0_fun/ppermute | solution.py:312
  36.2 2.9 %collective-permute-done.rest_1_ = bf16[20,32,128]{2,1,0:T(8,128)(2,1)S(1)} collective-permute-done((bf16[20,32,128]{2,1,0:T(8,128)(2,1)S(1)}, bf16[20,32,128]{2,1,0:T(8,128)(2,1)S(1)}, u32[]{:S(2)}, u32[]{:S(2)}) %collective-permute-start) | collective-permute-done | bytes 163872 | tf_op jit(solution)/shard_map/cond/branch_0_fun/ppermute | solution.py:312
  39.1 4.7 %collective-permute-done.1.rest_2_ = bf16[20,32,128]{2,1,0:T(8,128)(2,1)S(1)} collective-permute-done((bf16[20,32,128]{2,1,0:T(8,128)(2,1)S(1)}, bf16[20,32,128]{2,1,0:T(8,128)(2,1)S(1)}, u32[]{:S(2)}, u32[]{:S(2)}) %collective-permute-start.1) | collective-permute-done | bytes 163872 | tf_op jit(solution)/shard_map/cond/branch_0_fun/ppermute | solution.py:312
  43.8 6.4 %coef_join.3.after.coef = bf16[80,128,128]{2,1,0:T(8,128)(2,1)S(1)} custom-call(s32[2]{0:T(128)S(1)} %get-tuple-element.86.after.me, s32[320]{0:T(512)S(1)} %sub.69.pos, bf16[20,32,128]{2,1,0:T(8,128)(2,1)S(1)} %get-tuple-element.104.rest_0_, bf16[20,32,128]{2,1,0:T(8,128)(2,1)S(1)} %collective-permute-done.rest_1_, ...), custom_call_target="tpu_custom_call" | custom-call | bytes 4194304 | tf_op jit(solution)/shard_map/cond/branch_0_fun/coef_join/pallas_call | solution.py:80
  51.5 3.0 %tile_pick.7 = (bf16[32,5,32,128]{3,2,1,0:T(8,128)(2,1)S(1)}, s32[1]{0:T(128)}) custom-call(s32[2]{0:T(128)S(1)} %get-tuple-element.93.at, s32[9]{0:T(128)S(1)} %get-tuple-element.94.listed, bf16[32,32,480]{2,1,0:T(8,128)(2,1)S(1)} %bitcast.53, bf16[32,32,480]{2,1,0:T(8,128)(2,1)} %bitcast.8.got, bf16[80,128,128]{2,1,0:T(8,128)(2,1)S(1)} %coef_join.3.after.coef), custom_call_target="tpu_custom_call" | custom-call | bytes 4194304 | tf_op jit(solution)/shard_map/cond/branch_0_fun/tile_pick/pallas_call | solution.py:162
  55.5 2.5 %all-to-all-done.1.got = bf16[32,5,32,128]{3,2,1,0:T(8,128)(2,1)} async-done(((bf16[32,5,32,128]{3,2,1,0:T(8,128)(2,1)}), bf16[32,5,32,128]{3,2,1,0:T(8,128)(2,1)}, u32[]{:S(2)}, u32[]{:S(2)}) %all-to-all-start.1) | async-done | bytes 1310752 | tf_op jit(solution)/shard_map/cond/branch_0_fun/all_to_all | solution.py:344
  58.0 8.3 %all-to-all-start = ((bf16[32,5,32,128]{3,2,1,0:T(8,128)(2,1)}), bf16[32,5,32,128]{3,2,1,0:T(8,128)(2,1)}, u32[]{:S(2)}, u32[]{:S(2)}) async-start(bf16[32,5,32,128]{3,2,1,0:T(8,128)(2,1)} %copy-done.2), calls=%async_computation | async-start | bytes 2621440 | tf_op jit(solution)/shard_map/cond/branch_0_fun/all_to_all | solution.py:344
  67.3 1.9 %slot_pick.6 = (bf16[20,32,128]{2,1,0:T(8,128)(2,1)S(1)}, bf16[20,32,128]{2,1,0:T(8,128)(2,1)S(1)}, bf16[20,32,128]{2,1,0:T(8,128)(2,1)S(1)}, bf16[20,32,128]{2,1,0:T(8,128)(2,1)S(1)}) custom-call(s32[2]{0:T(128)S(1)} %get-tuple-element.86.after.me, s32[160]{0:T(256)S(1)} %reshape.375.spots, bf16[32,5,32,128]{3,2,1,0:T(8,128)(2,1)} %all-to-all-done.1.got, ...), custom_call_target="tpu_custom_call" | custom-call | bytes 2097152 | tf_op jit(solution)/shard_map/cond/branch_0_fun/slot_pick/pallas_call | solution.py:194
  69.3 5.2 %collective-permute-start.5 = (bf16[20,32,128]{2,1,0:T(8,128)(2,1)S(1)}, bf16[20,32,128]{2,1,0:T(8,128)(2,1)S(1)}, u32[]{:S(2)}, u32[]{:S(2)}) collective-permute-start(bf16[20,32,128]{2,1,0:T(8,128)(2,1)S(1)} %get-tuple-element.117), channel_id=1, source_target_pairs={{0,2},{1,3},{2,0},{3,1},{4,6},{5,7},{6,4},{7,5},{8,10},{9,11},{10,... | collective-permute-start | bytes 491528 | tf_op jit(solution)/shard_map/cond/branch_0_fun/ppermute | solution.py:312
  74.5 2.7 %collective-permute-done.4.rest_1_ = bf16[20,32,128]{2,1,0:T(8,128)(2,1)S(1)} collective-permute-done((bf16[20,32,128]{2,1,0:T(8,128)(2,1)S(1)}, bf16[20,32,128]{2,1,0:T(8,128)(2,1)S(1)}, u32[]{:S(2)}, u32[]{:S(2)}) %collective-permute-start.4) | collective-permute-done | bytes 163872 | tf_op jit(solution)/shard_map/cond/branch_0_fun/ppermute | solution.py:312
  77.2 4.4 %collective-permute-done.5.rest_2_ = bf16[20,32,128]{2,1,0:T(8,128)(2,1)S(1)} collective-permute-done((bf16[20,32,128]{2,1,0:T(8,128)(2,1)S(1)}, bf16[20,32,128]{2,1,0:T(8,128)(2,1)S(1)}, u32[]{:S(2)}, u32[]{:S(2)}) %collective-permute-start.5) | collective-permute-done | bytes 163872 | tf_op jit(solution)/shard_map/cond/branch_0_fun/ppermute | solution.py:312
  81.7 3.3 %product0.3 = (bf16[2,1,80,128,128]{4,3,2,1,0:T(8,128)(2,1)}, s32[1]{0:T(128)}) custom-call(s32[2]{0:T(128)S(1)} %get-tuple-element.86.after.me, s32[320]{0:T(512)S(1)} %sub.69.pos, bf16[80,128,128]{2,1,0:T(8,128)(2,1)S(1)} %coef_join.3.after.coef, bf16[20,32,128]{2,1,0:T(8,128)(2,1)S(1)} %get-tuple-element.115.rest_0_, ...), custom_call_target="tpu_custom_call" | custom-call | flops 335544320 | bytes 6291456 | tf_op jit(solution)/shard_map/cond/branch_0_fun/product0/pallas_call | solution.py:228
  85.0 15.0 %all-to-all-done.got = bf16[32,5,32,128]{3,2,1,0:T(8,128)(2,1)} async-done(((bf16[32,5,32,128]{3,2,1,0:T(8,128)(2,1)}), bf16[32,5,32,128]{3,2,1,0:T(8,128)(2,1)}, u32[]{:S(2)}, u32[]{:S(2)}) %all-to-all-start) | async-done | bytes 1310752 | tf_op jit(solution)/shard_map/cond/branch_0_fun/all_to_all | solution.py:344
  100.1 2.5 %slot_pick.7 = (bf16[20,32,128]{2,1,0:T(8,128)(2,1)S(1)}, bf16[20,32,128]{2,1,0:T(8,128)(2,1)S(1)}, bf16[20,32,128]{2,1,0:T(8,128)(2,1)S(1)}, bf16[20,32,128]{2,1,0:T(8,128)(2,1)S(1)}) custom-call(s32[2]{0:T(128)S(1)} %get-tuple-element.86.after.me, s32[160]{0:T(256)S(1)} %reshape.375.spots, bf16[32,5,32,128]{3,2,1,0:T(8,128)(2,1)} %all-to-all-done.got, ...), custom_call_target="tpu_custom_call" | custom-call | bytes 2097152 | tf_op jit(solution)/shard_map/cond/branch_0_fun/slot_pick/pallas_call | solution.py:194
  102.7 5.5 %collective-permute-start.8 = (bf16[20,32,128]{2,1,0:T(8,128)(2,1)S(1)}, bf16[20,32,128]{2,1,0:T(8,128)(2,1)S(1)}, u32[]{:S(2)}, u32[]{:S(2)}) collective-permute-start(bf16[20,32,128]{2,1,0:T(8,128)(2,1)S(1)} %get-tuple-element.122), channel_id=1, source_target_pairs={{0,2},{1,3},{2,0},{3,1},{4,6},{5,7},{6,4},{7,5},{8,10},{9,11},{10,... | collective-permute-start | bytes 491528 | tf_op jit(solution)/shard_map/cond/branch_0_fun/ppermute | solution.py:312
  108.2 2.7 %collective-permute-done.7.rest_1_ = bf16[20,32,128]{2,1,0:T(8,128)(2,1)S(1)} collective-permute-done((bf16[20,32,128]{2,1,0:T(8,128)(2,1)S(1)}, bf16[20,32,128]{2,1,0:T(8,128)(2,1)S(1)}, u32[]{:S(2)}, u32[]{:S(2)}) %collective-permute-start.7) | collective-permute-done | bytes 163872 | tf_op jit(solution)/shard_map/cond/branch_0_fun/ppermute | solution.py:312
  110.9 4.1 %collective-permute-done.8.rest_2_ = bf16[20,32,128]{2,1,0:T(8,128)(2,1)S(1)} collective-permute-done((bf16[20,32,128]{2,1,0:T(8,128)(2,1)S(1)}, bf16[20,32,128]{2,1,0:T(8,128)(2,1)S(1)}, u32[]{:S(2)}, u32[]{:S(2)}) %collective-permute-start.8) | collective-permute-done | bytes 163872 | tf_op jit(solution)/shard_map/cond/branch_0_fun/ppermute | solution.py:312
  115.0 3.3 %product1.3 = (bf16[2,1,80,128,128]{4,3,2,1,0:T(8,128)(2,1)}, s32[1]{0:T(128)}) custom-call(s32[2]{0:T(128)S(1)} %get-tuple-element.86.after.me, s32[320]{0:T(512)S(1)} %sub.69.pos, bf16[80,128,128]{2,1,0:T(8,128)(2,1)S(1)} %coef_join.3.after.coef, bf16[20,32,128]{2,1,0:T(8,128)(2,1)S(1)} %get-tuple-element.120.rest_0_, ...), custom_call_target="tpu_custom_call", output_to_operand_aliasing={{0}: (7, {})} | custom-call | flops 335544320 | bytes 6291456 | tf_op jit(solution)/shard_map/cond/branch_0_fun/product1/pallas_call | solution.py:228
  (86 shorter events, 10.7 us)
Async XLA Ops:
  0.1 2.3 %copy-start.12 = (s32[320,2]{0,1:T(2,128)S(1)}, s32[320,2]{0,1:T(2,128)}, u32[]{:S(2)}) copy-start(s32[320,2]{0,1:T(2,128)} %param.12) | copy-start | bytes 7684
  0.1 2.4 %copy-start.14 = (s32[4,4]{1,0:T(4,128)S(1)}, s32[4,4]{1,0:T(4,128)}, u32[]{:S(2)}) copy-start(s32[4,4]{1,0:T(4,128)} %param.11) | copy-start | bytes 196
  0.1 2.5 %copy-start.13 = (s32[4,4,20]{2,1,0:T(4,128)S(1)}, s32[4,4,20]{2,1,0:T(4,128)}, u32[]{:S(2)}) copy-start(s32[4,4,20]{2,1,0:T(4,128)} %param.10) | copy-start | bytes 3844
  2.2 5.4 %collective-permute-start.30 = (bf16[8,4,32,480]{3,2,1,0:T(8,128)(2,1)S(1)}, bf16[8,4,32,480]{3,2,1,0:T(8,128)(2,1)S(1)}, u32[]{:S(2)}, u32[]{:S(2)}) collective-permute-start(bf16[8,4,32,480]{3,2,1,0:T(8,128)(2,1)S(1)} %get-tuple-element.220), channel_id=1, source_target_pairs={{0,4},{4,0},{1,5},{5,1},{2,6},{6,2},{3,7},{7,3},{8,12},{12,8},{9,1... | collective-permute-start | bytes 2949128 | tf_op jit(solution)/shard_map/ppermute | solution.py:270
  10.6 47.4 %all-to-all-start.1 = ((bf16[32,5,32,128]{3,2,1,0:T(8,128)(2,1)}), bf16[32,5,32,128]{3,2,1,0:T(8,128)(2,1)}, u32[]{:S(2)}, u32[]{:S(2)}) async-start(bf16[32,5,32,128]{3,2,1,0:T(8,128)(2,1)} %get-tuple-element.114), calls=%async_computation.1 | async-start | bytes 2621440 | tf_op jit(solution)/shard_map/cond/branch_0_fun/all_to_all | solution.py:344
  23.6 4.4 %copy-start.9 = (bf16[32,30720]{1,0:T(8,128)(2,1)S(1)}, bf16[32,30720]{1,0:T(8,128)(2,1)}, u32[]{:S(2)}) copy-start(bf16[32,30720]{1,0:T(8,128)(2,1)} %get-tuple-element.102.coef) | copy-start | bytes 5898244 | tf_op jit(solution)/shard_map/cond
  26.8 1.0 copy-start.3
  27.8 22.5 %collective-permute-start.3 = (bf16[8,4,32,480]{3,2,1,0:T(8,128)(2,1)}, bf16[8,4,32,480]{3,2,1,0:T(8,128)(2,1)}, u32[]{:S(2)}, u32[]{:S(2)}) collective-permute-start(bf16[8,4,32,480]{3,2,1,0:T(8,128)(2,1)} %get-tuple-element.112), channel_id=1, source_target_pairs={{0,4},{4,0},{1,5},{5,1},{2,6},{6,2},{3,7},{7,3},{8,12},{12,8},{9,1... | collective-permute-start | bytes 2949128 | tf_op jit(solution)/shard_map/cond/branch_0_fun/ppermute | solution.py:270
  29.6 9.5 %collective-permute-start = (bf16[20,32,128]{2,1,0:T(8,128)(2,1)S(1)}, bf16[20,32,128]{2,1,0:T(8,128)(2,1)S(1)}, u32[]{:S(2)}, u32[]{:S(2)}) collective-permute-start(bf16[20,32,128]{2,1,0:T(8,128)(2,1)S(1)} %get-tuple-element.105), channel_id=1, source_target_pairs={{0,1},{1,2},{2,3},{3,0},{4,5},{5,6},{6,7},{7,4},{8,9},{9,10},{10,1... | collective-permute-start | bytes 491528 | tf_op jit(solution)/shard_map/cond/branch_0_fun/ppermute | solution.py:312
  31.0 12.8 %collective-permute-start.1 = (bf16[20,32,128]{2,1,0:T(8,128)(2,1)S(1)}, bf16[20,32,128]{2,1,0:T(8,128)(2,1)S(1)}, u32[]{:S(2)}, u32[]{:S(2)}) collective-permute-start(bf16[20,32,128]{2,1,0:T(8,128)(2,1)S(1)} %get-tuple-element.106), channel_id=1, source_target_pairs={{0,2},{1,3},{2,0},{3,1},{4,6},{5,7},{6,4},{7,5},{8,10},{9,11},{10,... | collective-permute-start | bytes 491528 | tf_op jit(solution)/shard_map/cond/branch_0_fun/ppermute | solution.py:312
  35.7 8.1 %collective-permute-start.2 = (bf16[20,32,128]{2,1,0:T(8,128)(2,1)S(1)}, bf16[20,32,128]{2,1,0:T(8,128)(2,1)S(1)}, u32[]{:S(2)}, u32[]{:S(2)}) collective-permute-start(bf16[20,32,128]{2,1,0:T(8,128)(2,1)S(1)} %get-tuple-element.107), channel_id=1, source_target_pairs={{0,3},{1,0},{2,1},{3,2},{4,7},{5,4},{6,5},{7,6},{8,11},{9,8},{10,9... | collective-permute-start | bytes 491528 | tf_op jit(solution)/shard_map/cond/branch_0_fun/ppermute | solution.py:312
  50.2 1.2 %copy-start.4 = (bf16[8,4,32,480]{3,2,1,0:T(8,128)(2,1)S(1)}, bf16[8,4,32,480]{3,2,1,0:T(8,128)(2,1)}, u32[]{:S(2)}) copy-start(bf16[8,4,32,480]{3,2,1,0:T(8,128)(2,1)} %copy-done.3) | copy-start | bytes 2949124 | tf_op jit(solution)/shard_map/cond
  54.4 1.1 copy-start.2
  58.0 42.1 %all-to-all-start = ((bf16[32,5,32,128]{3,2,1,0:T(8,128)(2,1)}), bf16[32,5,32,128]{3,2,1,0:T(8,128)(2,1)}, u32[]{:S(2)}, u32[]{:S(2)}) async-start(bf16[32,5,32,128]{3,2,1,0:T(8,128)(2,1)} %copy-done.2), calls=%async_computation | async-start | bytes 2621440 | tf_op jit(solution)/shard_map/cond/branch_0_fun/all_to_all | solution.py:344
  69.2 8.0 %collective-permute-start.4 = (bf16[20,32,128]{2,1,0:T(8,128)(2,1)S(1)}, bf16[20,32,128]{2,1,0:T(8,128)(2,1)S(1)}, u32[]{:S(2)}, u32[]{:S(2)}) collective-permute-start(bf16[20,32,128]{2,1,0:T(8,128)(2,1)S(1)} %get-tuple-element.116), channel_id=1, source_target_pairs={{0,1},{1,2},{2,3},{3,0},{4,5},{5,6},{6,7},{7,4},{8,9},{9,10},{10,1... | collective-permute-start | bytes 491528 | tf_op jit(solution)/shard_map/cond/branch_0_fun/ppermute | solution.py:312
  69.3 12.3 %collective-permute-start.5 = (bf16[20,32,128]{2,1,0:T(8,128)(2,1)S(1)}, bf16[20,32,128]{2,1,0:T(8,128)(2,1)S(1)}, u32[]{:S(2)}, u32[]{:S(2)}) collective-permute-start(bf16[20,32,128]{2,1,0:T(8,128)(2,1)S(1)} %get-tuple-element.117), channel_id=1, source_target_pairs={{0,2},{1,3},{2,0},{3,1},{4,6},{5,7},{6,4},{7,5},{8,10},{9,11},{10,... | collective-permute-start | bytes 491528 | tf_op jit(solution)/shard_map/cond/branch_0_fun/ppermute | solution.py:312
  74.5 7.2 %collective-permute-start.6 = (bf16[20,32,128]{2,1,0:T(8,128)(2,1)S(1)}, bf16[20,32,128]{2,1,0:T(8,128)(2,1)S(1)}, u32[]{:S(2)}, u32[]{:S(2)}) collective-permute-start(bf16[20,32,128]{2,1,0:T(8,128)(2,1)S(1)} %get-tuple-element.118), channel_id=1, source_target_pairs={{0,3},{1,0},{2,1},{3,2},{4,7},{5,4},{6,5},{7,6},{8,11},{9,8},{10,9... | collective-permute-start | bytes 491528 | tf_op jit(solution)/shard_map/cond/branch_0_fun/ppermute | solution.py:312
  102.6 8.3 %collective-permute-start.7 = (bf16[20,32,128]{2,1,0:T(8,128)(2,1)S(1)}, bf16[20,32,128]{2,1,0:T(8,128)(2,1)S(1)}, u32[]{:S(2)}, u32[]{:S(2)}) collective-permute-start(bf16[20,32,128]{2,1,0:T(8,128)(2,1)S(1)} %get-tuple-element.121), channel_id=1, source_target_pairs={{0,1},{1,2},{2,3},{3,0},{4,5},{5,6},{6,7},{7,4},{8,9},{9,10},{10,1... | collective-permute-start | bytes 491528 | tf_op jit(solution)/shard_map/cond/branch_0_fun/ppermute | solution.py:312
  102.7 12.3 %collective-permute-start.8 = (bf16[20,32,128]{2,1,0:T(8,128)(2,1)S(1)}, bf16[20,32,128]{2,1,0:T(8,128)(2,1)S(1)}, u32[]{:S(2)}, u32[]{:S(2)}) collective-permute-start(bf16[20,32,128]{2,1,0:T(8,128)(2,1)S(1)} %get-tuple-element.122), channel_id=1, source_target_pairs={{0,2},{1,3},{2,0},{3,1},{4,6},{5,7},{6,4},{7,5},{8,10},{9,11},{10,... | collective-permute-start | bytes 491528 | tf_op jit(solution)/shard_map/cond/branch_0_fun/ppermute | solution.py:312
  108.2 6.8 %collective-permute-start.9 = (bf16[20,32,128]{2,1,0:T(8,128)(2,1)S(1)}, bf16[20,32,128]{2,1,0:T(8,128)(2,1)S(1)}, u32[]{:S(2)}, u32[]{:S(2)}) collective-permute-start(bf16[20,32,128]{2,1,0:T(8,128)(2,1)S(1)} %get-tuple-element.123), channel_id=1, source_target_pairs={{0,3},{1,0},{2,1},{3,2},{4,7},{5,4},{6,5},{7,6},{8,11},{9,8},{10,9... | collective-permute-start | bytes 491528 | tf_op jit(solution)/shard_map/cond/branch_0_fun/ppermute | solution.py:312
